TPU v7x, 32 devices: a whole 2x2x4 slice. The times are simulated.
32 devices in a mesh: depth: 8 (over z, x), stripe: 4 (over y, core).
Axes of the slice: x: 2, y: 2, z: 4, core: 2. Of those that a mesh axis runs over, the one named last changes fastest.
Arguments:
- object_slices: float32 [8, 2, 1024, 384], P('depth', None, 'stripe'), may hold values from -1 to 1, as said below
- probe_wave: bfloat16 [2, 256, 256], replicated, may hold values from -5 to 5
- amplitudes: bfloat16 [16, 256, 256], P('stripe'), may hold values from 0 to 2
- positions: int32 [16, 2], replicated, may hold values from 0 to 255, as said below
- counts: int32 [4], replicated, may hold values from 1 to 4, as said below
Outputs:
- grad_object: float32 [8, 2, 1024, 384], P('depth', None, 'stripe')
Inputs may be any that keep to these rules, and one draw needn't show every extreme that they name: `object_slices`: every cell has magnitude at most 1. `positions`: row offsets lie in 0 to 255 and column offsets in 0 to 128. The counts sum to 8 and the largest equals 4; a stripe's live slots are its first ones.
All inputs are finite; a program needn't handle non-finite values.
Results may differ from a plain program's by a relative error of at most 0.0003.
Values may be sent and summed in bfloat16 or wider, within the bound.
A program may use at most 64 MiB of HBM per device.

v0:
```python
import functools

import jax
import jax.numpy as jnp
import numpy as np
from jax import lax
from jax.experimental import pallas as pl
from jax.experimental.pallas import tpu as pltpu
from jax.sharding import PartitionSpec as P

smoothing = 0.25
LEVELS = 32767.0
MESH = pl.DeviceIdType.MESH


def right_form(matrix):
    return np.block([[matrix.real, matrix.imag], [-matrix.imag, matrix.real]])


def make_tables(length):
    half = length // 2
    index = np.arange(length)
    dft = np.exp(-2j * np.pi * (np.outer(index, index) % length) / length) / np.sqrt(length)
    freq = (index + half) % length - half
    fresnel = np.exp(-1j * np.pi * freq.astype(np.float64) ** 2 / (2.0 * length))
    prop = dft.conj() @ (fresnel[:, None] * dft)
    first, second = prop[:half, :half], prop[:half, half:]
    parts = [(first + second) / 2, (first - second) / 2, dft[:half, 0::2], dft[:half, 1::2]]
    tables = []
    for part in parts:
        right = right_form(part)
        tables += [right, right.T]
    stacked = np.stack(tables).astype(np.float32)
    high = stacked.astype(jnp.bfloat16)
    low = (stacked - high.astype(np.float32)).astype(jnp.bfloat16)
    order = np.concatenate([np.arange(0, length, 2), np.arange(1, length, 2)])
    pick = np.zeros((length, length), np.float32)
    pick[np.arange(length), order] = 1.0
    picks = np.stack([pick, pick.T]).astype(jnp.bfloat16)
    return np.concatenate([high, low, picks], axis=0)


def parts_of(value):
    high = value.astype(jnp.bfloat16)
    low = (value - high.astype(jnp.float32)).astype(jnp.bfloat16)
    return high, low


def dot(a, b):
    return jnp.dot(a, b, preferred_element_type=jnp.float32)


def kernel(
    depth_count, stripe_count, capacity, positions_ref, counts_ref, object_ref, probe_ref, amp_ref,
    table_hbm, out_ref,
    slab_re, slab_im, win, wins, waves, gout, gscale, gin, gin_scale, rstack, lstack, adj_buf,
    table_ref, table_sem, patterns, across, across_scale, given, given_scale,
    send_n, recv_n, send_w, recv_w, send_g, recv_g, send_s, recv_s, send_h, send_hs, send_a, recv_a,
    send_f, recv_f, send_fs, recv_fs,
):
    me = lax.axis_index("depth")
    stripe = lax.axis_index("stripe")
    share = capacity // 2
    stride = depth_count // (share + 2)
    slabs = (slab_re, slab_im)
    length = probe_ref.shape[-1]
    half = length // 2
    count = (table_ref.shape[0] - 2) // 2
    partner = stripe + 1 - 2 * lax.rem(stripe, 2)
    opposite = lax.rem(stripe + 2, stripe_count)

    def slot_of(place):
        owner, passed, start = jnp.int32(0), jnp.int32(0), jnp.int32(0)
        for other in range(1, stripe_count):
            passed = passed + counts_ref[other - 1]
            owner = owner + jnp.where(place >= passed, 1, 0)
            start = jnp.where(place >= passed, passed, start)
        within = jnp.clip(place - start, 0, capacity - 1)
        slot = owner * capacity + within
        return owner, within, positions_ref[0, slot], positions_ref[1, slot]

    share_base = jnp.maximum(me - lax.rem(stripe, 2), 0)
    my_slot = jnp.clip(share_base // stride - 1, 0, share - 1)
    is_worker = me == (my_slot + 1) * stride + lax.rem(stripe, 2)

    @pl.when(is_worker)
    def _():
        pltpu.make_async_copy(table_hbm, table_ref, table_sem).start()

    barrier = pltpu.get_barrier_semaphore()

    @pl.loop(1, depth_count)
    def greet(step):
        other = lax.rem(me + step, depth_count)
        pl.semaphore_signal(barrier, inc=1, device_id=(other, stripe), device_id_type=MESH)

    for step in range(1, stripe_count):
        other = lax.rem(stripe + step, stripe_count)
        pl.semaphore_signal(barrier, inc=1, device_id=(me, other), device_id_type=MESH)
    for part in range(2):
        whole = jnp.round(object_ref[0, part] * LEVELS).astype(jnp.int32)
        slabs[part][stripe] = whole.astype(jnp.int16)
    pl.semaphore_wait(barrier, depth_count + stripe_count - 2)

    def slab_copy(route, part):
        source = opposite if route == 2 else stripe
        target = opposite if route == 1 else partner
        return pltpu.make_async_remote_copy(
            src_ref=slabs[part].at[source], dst_ref=slabs[part].at[source],
            send_sem=send_n.at[route, part], recv_sem=recv_n.at[route, part],
            device_id=(me, target), device_id_type=MESH,
        )

    for part in range(2):
        slab_copy(1, part).start()
        slab_copy(0, part).start()

    def worker_of(slot):
        return (slot + 1) * stride + lax.rem(stripe, 2)

    my_owner, my_within, my_row, my_col = slot_of(stripe * share + my_slot)

    def pattern_copy(parity, turn):
        return pltpu.make_async_remote_copy(
            src_ref=amp_ref, dst_ref=patterns.at[stripe], send_sem=send_a.at[turn],
            recv_sem=recv_a.at[stripe], device_id=(me, 2 * turn + parity), device_id_type=MESH,
        )

    def each_pattern_target(action):
        for parity in range(2):
            for slot in range(share):
                for turn in range(stripe_count // 2):
                    here = (me == (slot + 1) * stride + parity) & (stripe != 2 * turn + parity)

                    @pl.when(here)
                    def _():
                        action(pattern_copy(parity, turn))

    each_pattern_target(lambda copy: copy.start())

    for part in range(2):
        slab_copy(1, part).wait_recv()
        slab_copy(2, part).start()

    @pl.when(is_worker)
    def _():
        pltpu.make_async_copy(table_hbm, table_ref, table_sem).wait()
        for which in range(count // 2):
            high, low = table_ref[2 * which], table_ref[count + 2 * which]
            rstack[which] = jnp.concatenate([high, low, high], axis=0)
            high, low = table_ref[2 * which + 1], table_ref[count + 2 * which + 1]
            lstack[which] = jnp.concatenate([high, low, high], axis=1)
        gscale[...] = jnp.zeros(gscale.shape, jnp.float32)
        pltpu.make_async_copy(amp_ref, patterns.at[stripe], recv_a.at[stripe]).start()
        first = lax.broadcasted_iota(jnp.int32, (length, length), 0)
        second = lax.broadcasted_iota(jnp.int32, (length, length), 1)
        turned = second + my_row
        turned = jnp.where(turned >= length, turned - length, turned)
        turn_rows = jnp.where(first == turned, 1.0, 0.0).astype(jnp.bfloat16)
        turned = first + my_col
        turned = jnp.where(turned >= length, turned - length, turned)
        turn_cols = jnp.where(second == turned, 1.0, 0.0).astype(jnp.bfloat16)
        for part in range(2):
            value = dot(turn_rows, probe_ref[part]).astype(jnp.bfloat16)
            waves[0, part] = dot(value, turn_cols)

    def window_copy(slot, part, target):
        return pltpu.make_async_remote_copy(
            src_ref=win.at[slot, part], dst_ref=wins.at[me, part], send_sem=send_w.at[slot, part],
            recv_sem=recv_w.at[me, part], device_id=(target, stripe), device_id_type=MESH,
        )

    row_index = lax.broadcasted_iota(jnp.int32, (length, half), 0)
    col_index = lax.broadcasted_iota(jnp.int32, (length, half), 1)
    for part in range(2):
        slab_copy(0, part).wait_recv()
        slab_copy(2, part).wait_recv()
        for slot in range(share):
            owner, _, row, col = slot_of(stripe * share + slot)
            later = lax.rem(owner + 1, stripe_count)
            here = row_index >= row
            near = col_index >= col
            left, mid, right = (
                jnp.where(
                    here,
                    slabs[part][owner, :, pl.ds(place * half, half)].astype(jnp.int32),
                    slabs[part][later, :, pl.ds(place * half, half)].astype(jnp.int32),
                )
                for place in range(3)
            )
            win[slot, part, :, pl.ds(0, half)] = jnp.where(near, left, right).astype(jnp.int16)
            win[slot, part, :, pl.ds(half, half)] = mid.astype(jnp.int16)
            target = worker_of(slot)

            @pl.when(me != target)
            def _():
                window_copy(slot, part, target).start()

            @pl.when(me == target)
            def _():
                pltpu.make_async_copy(
                    win.at[slot, part], wins.at[me, part], recv_w.at[me, part]
                ).start()

    def wait_window(layer):
        for part in range(2):
            pltpu.make_async_copy(
                win.at[0, part], wins.at[layer, part], recv_w.at[layer, part]
            ).wait()

    def grad_copy(layer, part):
        return pltpu.make_async_remote_copy(
            src_ref=gout.at[layer, part], dst_ref=gin.at[my_slot, part],
            send_sem=send_g.at[layer, part], recv_sem=recv_g.at[my_slot, part], device_id=(layer, stripe), device_id_type=MESH,
        )

    def scale_copy(layer, part):
        return pltpu.make_async_remote_copy(
            src_ref=gscale.at[layer, part], dst_ref=gin_scale.at[my_slot, part],
            send_sem=send_s.at[layer, part], recv_sem=recv_s.at[my_slot, part], device_id=(layer, stripe), device_id_type=MESH,
        )

    def right_dot(value, which):
        high, low = parts_of(value)
        return dot(jnp.concatenate([high, high, low], axis=1), rstack[which])

    def left_dot(which, value):
        high, low = parts_of(value)
        return dot(lstack[which], jnp.concatenate([high, high, low], axis=0))

    def split_lanes(re, im):
        return (
            jnp.concatenate([re[:, :half] + re[:, half:], im[:, :half] + im[:, half:]], axis=1),
            jnp.concatenate([re[:, :half] - re[:, half:], im[:, :half] - im[:, half:]], axis=1),
        )

    def split_rows(re, im):
        return (
            jnp.concatenate([re[:half] + re[half:], im[:half] + im[half:]], axis=0),
            jnp.concatenate([re[:half] - re[half:], im[:half] - im[half:]], axis=0),
        )

    def join_lanes(p, q):
        return (
            jnp.concatenate([p[:, :half] + q[:, :half], p[:, :half] - q[:, :half]], axis=1),
            jnp.concatenate([p[:, half:] + q[:, half:], p[:, half:] - q[:, half:]], axis=1),
        )

    def join_rows(p, q):
        return (
            jnp.concatenate([p[:half] + q[:half], p[:half] - q[:half]], axis=0),
            jnp.concatenate([p[half:] + q[half:], p[half:] - q[half:]], axis=0),
        )

    def propagate(re, im):
        u, v = split_lanes(re, im)
        re, im = join_lanes(right_dot(u, 0), right_dot(v, 1))
        u, v = split_rows(re, im)
        return join_rows(left_dot(0, u), left_dot(1, v))

    def window_of(layer):
        value = wins[layer].astype(jnp.int32).astype(jnp.float32) * (1.0 / LEVELS)
        return value[0], value[1]

    def emit(layer, re, im):
        for part, value in enumerate((re, im)):
            most = jnp.max(jnp.abs(value), axis=0, keepdims=True)
            most = jnp.maximum(most, 1e-30)
            gout[layer, part] = jnp.round(value * (LEVELS / most)).astype(jnp.int32).astype(jnp.int16)
            gscale[layer, part, pl.ds(0, 1), :] = most * (1.0 / LEVELS)

            @pl.when(layer != me)
            def _():
                grad_copy(layer, part).start()
                scale_copy(layer, part).start()

            @pl.when(layer == me)
            def _():
                pltpu.make_async_copy(
                    gout.at[layer, part], gin.at[my_slot, part], recv_g.at[my_slot, part]
                ).start()
                pltpu.make_async_copy(
                    gscale.at[layer, part], gin_scale.at[my_slot, part], recv_s.at[my_slot, part]
                ).start()

    @pl.when(is_worker)
    def _():
        @pl.loop(0, depth_count - 1)
        def forward(layer):
            wait_window(layer)
            win_re, win_im = window_of(layer)
            re, im = waves[layer, 0], waves[layer, 1]
            re, im = propagate(re * win_re - im * win_im, re * win_im + im * win_re)
            waves[layer + 1, 0] = re
            waves[layer + 1, 1] = im

        last = depth_count - 1
        wait_window(last)
        win_re, win_im = window_of(last)
        wave_re, wave_im = waves[last, 0], waves[last, 1]
        re = wave_re * win_re - wave_im * win_im
        im = wave_re * win_im + wave_im * win_re
        u, v = split_lanes(re, im)
        even, odd = right_dot(u, 2), right_dot(v, 3)
        re = jnp.concatenate([even[:, :half], odd[:, :half]], axis=1)
        im = jnp.concatenate([even[:, half:], odd[:, half:]], axis=1)
        u, v = split_rows(re, im)
        even, odd = left_dot(2, u), left_dot(3, v)
        for source in range(stripe_count):
            pltpu.make_async_copy(amp_ref, patterns.at[source], recv_a.at[source]).wait()
        pick_rows, pick_cols = table_ref[2 * count], table_ref[2 * count + 1]
        amp = dot(dot(pick_rows, patterns[my_owner, my_within]).astype(jnp.bfloat16), pick_cols)
        re = jnp.concatenate([even[:half], odd[:half]], axis=0)
        im = jnp.concatenate([even[half:], odd[half:]], axis=0)
        factor = 1.0 - amp / jnp.sqrt(re * re + im * im + smoothing)
        re, im = factor * re, factor * im
        def left_back(which, value):
            high, low = parts_of(value)
            table = table_ref[2 * which]
            table_low = table_ref[count + 2 * which]
            return dot(table, high) + dot(table_low, high) + dot(table, low)

        def right_back(value, which):
            high, low = parts_of(value)
            table = table_ref[2 * which + 1]
            table_low = table_ref[count + 2 * which + 1]
            return dot(high, table) + dot(high, table_low) + dot(low, table)

        re, im = join_rows(
            left_back(2, jnp.concatenate([re[:half], im[:half]], axis=0)),
            left_back(3, jnp.concatenate([re[half:], im[half:]], axis=0)),
        )
        mid_re, mid_im = join_lanes(
            right_back(jnp.concatenate([re[:, :half], im[:, :half]], axis=1), 2),
            right_back(jnp.concatenate([re[:, half:], im[:, half:]], axis=1), 3),
        )
        emit(
            last,
            wave_re * mid_re + wave_im * mid_im,
            wave_re * mid_im - wave_im * mid_re,
        )
        adj_buf[0] = win_re * mid_re + win_im * mid_im
        adj_buf[1] = win_im * mid_re - win_re * mid_im

        @pl.loop(1, depth_count)
        def backward(step):
            layer = last - step
            mid_re, mid_conj = propagate(adj_buf[0], adj_buf[1])
            win_re, win_im = window_of(layer)
            wave_re, wave_im = waves[layer, 0], waves[layer, 1]
            emit(
                layer,
                wave_re * mid_re - wave_im * mid_conj,
                -(wave_re * mid_conj + wave_im * mid_re),
            )
            adj_buf[0] = win_re * mid_re - win_im * mid_conj
            adj_buf[1] = win_im * mid_re + win_re * mid_conj

    def across_copy(part):
        return pltpu.make_async_remote_copy(
            src_ref=across.at[part], dst_ref=given.at[part], send_sem=send_f.at[part],
            recv_sem=recv_f.at[part], device_id=(me, opposite), device_id_type=MESH,
        )

    def across_scale_copy(part):
        return pltpu.make_async_remote_copy(
            src_ref=across_scale.at[part], dst_ref=given_scale.at[part],
            send_sem=send_fs.at[part], recv_sem=recv_fs.at[part], device_id=(me, opposite),
            device_id_type=MESH,
        )

    def share_copy(slot, part):
        return pltpu.make_async_remote_copy(
            src_ref=gin.at[slot, part], dst_ref=gin.at[share + slot, part],
            send_sem=send_h.at[slot, part], recv_sem=recv_g.at[share + slot, part],
            device_id=(me, partner), device_id_type=MESH,
        )

    def share_scale_copy(slot, part):
        return pltpu.make_async_remote_copy(
            src_ref=gin_scale.at[slot, part], dst_ref=gin_scale.at[share + slot, part],
            send_sem=send_hs.at[slot, part], recv_sem=recv_s.at[share + slot, part],
            device_id=(me, partner), device_id_type=MESH,
        )

    across_scale[...] = jnp.zeros(across_scale.shape, jnp.float32)
    places = [stripe * share + slot for slot in range(share)]
    places += [partner * share + slot for slot in range(share)]
    for part in range(2):
        for slot in range(share):
            pltpu.make_async_copy(
                gout.at[0, part], gin.at[slot, part], recv_g.at[slot, part]
            ).wait()
            share_copy(slot, part).start()
            pltpu.make_async_copy(
                gscale.at[0, part], gin_scale.at[slot, part], recv_s.at[slot, part]
            ).wait()
            share_scale_copy(slot, part).start()
        for slot in range(share):
            share_copy(slot, part).wait_recv()
            share_scale_copy(slot, part).wait_recv()
        own_sums, far_sums = [0.0] * 3, [0.0] * 3
        for slot in range(2 * share):
            owner, _, row, col = slot_of(places[slot])
            later = lax.rem(owner + 1, stripe_count)
            here = row_index >= row
            near = col_index >= col
            scale = gin_scale[slot, part, pl.ds(0, 1), :]
            left = gin[slot, part, :, pl.ds(0, half)].astype(jnp.int32).astype(jnp.float32)
            left = left * scale[:, :half]
            mid = gin[slot, part, :, pl.ds(half, half)].astype(jnp.int32).astype(jnp.float32)
            mid = mid * scale[:, half:]
            pieces = (jnp.where(near, left, 0.0), mid, jnp.where(near, 0.0, left))
            gain = [
                jnp.where(
                    here,
                    jnp.where(owner == target, 1.0, 0.0),
                    jnp.where(later == target, 1.0, 0.0),
                )
                for target in (stripe, opposite)
            ]
            for place, piece in enumerate(pieces):
                own_sums[place] = own_sums[place] + piece * gain[0]
                far_sums[place] = far_sums[place] + piece * gain[1]
        for place in range(3):
            lanes = pl.ds(place * half, half)
            most = jnp.max(jnp.abs(far_sums[place]), axis=0, keepdims=True)
            most = jnp.maximum(most, 1e-30)
            whole = jnp.round(far_sums[place] * (LEVELS / most)).astype(jnp.int32)
            across[part, :, lanes] = whole.astype(jnp.int16)
            across_scale[part, pl.ds(0, 1), lanes] = most * (1.0 / LEVELS)
            out_ref[0, part, :, lanes] = own_sums[place]
        across_copy(part).start()
        across_scale_copy(part).start()

    for part in range(2):
        across_copy(part).wait_recv()
        across_scale_copy(part).wait_recv()
        value = given[part].astype(jnp.int32).astype(jnp.float32)
        out_ref[0, part] += value * given_scale[part, pl.ds(0, 1), :]

    for part in range(2):
        for route in range(3):
            slab_copy(route, part).wait_send()
        across_copy(part).wait_send()
        across_scale_copy(part).wait_send()
    each_pattern_target(lambda copy: copy.wait_send())
    for slot in range(share):
        for part in range(2):
            share_copy(slot, part).wait_send()
            share_scale_copy(slot, part).wait_send()
        target = worker_of(slot)

        @pl.when(me != target)
        def _():
            for part in range(2):
                window_copy(slot, part, target).wait_send()

    @pl.when(is_worker)
    def _():
        @pl.loop(0, depth_count)
        def drain(layer):
            @pl.when(layer != me)
            def _():
                for part in range(2):
                    grad_copy(layer, part).wait_send()
                    scale_copy(layer, part).wait_send()


def body(tables, object_slices, probe_wave, amplitudes, positions, counts):
    stripe_count = lax.axis_size("stripe")
    depth_count = lax.axis_size("depth")
    layers, _, stripe_rows, width = object_slices.shape
    length = probe_wave.shape[1]
    capacity = amplitudes.shape[0]
    assert layers == 1 and stripe_rows == length and 2 * width == 3 * length
    share = capacity // 2
    assert depth_count >= 2 * (share + 2) and stripe_count == 4 and capacity % 2 == 0

    field = (2, length, length)
    slab = (2, stripe_rows, width)
    slab_scale = (2, 8, width)
    vmem = pl.BlockSpec(memory_space=pltpu.VMEM)
    smem = pl.BlockSpec(memory_space=pltpu.SMEM)
    dma = pltpu.SemaphoreType.DMA
    count = (tables.shape[0] - 2) // 4
    return pl.pallas_call(
        functools.partial(kernel, depth_count, stripe_count, capacity),
        out_shape=jax.ShapeDtypeStruct(object_slices.shape, jnp.float32),
        in_specs=[smem] * 2 + [vmem] * 3 + [pl.BlockSpec(memory_space=pl.ANY)],
        out_specs=vmem,
        scratch_shapes=[
            pltpu.VMEM((stripe_count, stripe_rows, width), jnp.int16),
            pltpu.VMEM((stripe_count, stripe_rows, width), jnp.int16),
            pltpu.VMEM((share,) + field, jnp.int16),
            pltpu.VMEM((depth_count,) + field, jnp.int16),
            pltpu.VMEM((depth_count,) + field, jnp.float32),
            pltpu.VMEM((depth_count,) + field, jnp.int16),
            pltpu.VMEM((depth_count, 2, 8, length), jnp.float32),
            pltpu.VMEM((2 * share,) + field, jnp.int16),
            pltpu.VMEM((2 * share, 2, 8, length), jnp.float32),
            pltpu.VMEM((count, 3 * length, length), jnp.bfloat16),
            pltpu.VMEM((count, length, 3 * length), jnp.bfloat16),
            pltpu.VMEM(field, jnp.float32),
            pltpu.VMEM(tables.shape, tables.dtype),
            dma,
            pltpu.VMEM((stripe_count,) + amplitudes.shape, amplitudes.dtype),
            pltpu.VMEM(slab, jnp.int16),
            pltpu.VMEM(slab_scale, jnp.float32),
            pltpu.VMEM(slab, jnp.int16),
            pltpu.VMEM(slab_scale, jnp.float32),
            dma((3, 2)),
            dma((3, 2)),
            dma((share, 2)),
            dma((depth_count, 2)),
            dma((depth_count, 2)),
            dma((2 * share, 2)),
            dma((depth_count, 2)),
            dma((2 * share, 2)),
            dma((share, 2)),
            dma((share, 2)),
            dma((stripe_count // 2,)),
            dma((stripe_count,)),
            dma((2,)),
            dma((2,)),
            dma((2,)),
            dma((2,)),
        ],
        compiler_params=pltpu.CompilerParams(
            collective_id=0, has_side_effects=True, vmem_limit_bytes=60 * 1024 * 1024
        ),
    )(positions.T, counts, object_slices, probe_wave, amplitudes, tables)


def solution(mesh):
    def run(object_slices, probe_wave, amplitudes, positions, counts):
        tables = jnp.asarray(make_tables(probe_wave.shape[1]))
        return jax.shard_map(
            body,
            mesh=mesh,
            in_specs=(P(), P("depth", None, "stripe", None), P(), P("stripe", None, None), P(), P()),
            out_specs=P("depth", None, "stripe", None),
            check_vma=False,
        )(tables, object_slices, probe_wave, amplitudes, positions, counts)

    return run
```

profile of v0, /device:TPU:1, one launch (start us, length us, event | category | flops | bytes accessed | tf_op | source)
XLA Modules:
  0.0 71.4 jit_solution(12635436178370612446)
XLA Ops:
  0.0 69.3 %shard_map.64 = f32[1,2,256,384]{3,2,1,0:T(8,128)} custom-call(s32[2,16]{1,0:T(2,128)} %bitcast.1, s32[4]{0:T(128)} %counts_ref.1, f32[1,2,256,384]{3,2,1,0:T(8,128)} %object_ref.1, bf16[2,256,256]{2,1,0:T(8,128)(2,1)} %probe_ref.1, bf16[4,256,256]{2,1,0:T(8,128)(2,1)} %amp_ref.1, bf16[18,256,256]{2,1,0:T(8,128)(2,1)} %constant.2.clone.table_hbm), custom_call_target="tpu_custom_call" | custom-call | tf_op jit(solution)/shard_map/pallas_call | solution.py:487
  69.3 2.1 %copy.8 = f32[1,2,256,384]{3,2,1,0:T(8,128)} copy(f32[1,2,256,384]{3,2,1,0:T(8,128)} %shard_map.64) | data formatting | bytes 1572864
where the time goes:
time: 71.6 us; the launch traced here: 71.4 us
  Pallas kernels  69.3 us (97%)
  local copies, waits for them, and re-layouts  2.06 us (3%)
    pallas_call x1, Pallas kernels, body(): pl.pallas_call(functools.partial(kernel, depth_count, stripe_count, capac...  69.3 us
    unnamed x1, local copies, waits for them, and re-layouts  2.06 us

commit v1 on v0

v1 whole, which is shorter than its diff:
```python
import functools
import types

import jax
import jax.numpy as jnp
import numpy as np
from jax import lax
from jax.experimental import pallas as pl
from jax.experimental.pallas import tpu as pltpu
from jax.sharding import PartitionSpec as P

smoothing = 0.25
LEVELS = 32767.0
CHUNKS = 4
MESH = pl.DeviceIdType.MESH


def right_form(matrix):
    return np.block([[matrix.real, matrix.imag], [-matrix.imag, matrix.real]])


def make_tables(length):
    half = length // 2
    index = np.arange(length)
    dft = np.exp(-2j * np.pi * (np.outer(index, index) % length) / length) / np.sqrt(length)
    freq = (index + half) % length - half
    fresnel = np.exp(-1j * np.pi * freq.astype(np.float64) ** 2 / (2.0 * length))
    prop = dft.conj() @ (fresnel[:, None] * dft)
    first, second = prop[:half, :half], prop[:half, half:]
    parts = [(first + second) / 2, (first - second) / 2, dft[:half, 0::2], dft[:half, 1::2]]
    tables = []
    for part in parts:
        right = right_form(part)
        tables += [right, right.T]
    stacked = np.stack(tables).astype(np.float32)
    high = stacked.astype(jnp.bfloat16)
    low = (stacked - high.astype(np.float32)).astype(jnp.bfloat16)
    order = np.concatenate([np.arange(0, length, 2), np.arange(1, length, 2)])
    pick = np.zeros((length, length), np.float32)
    pick[np.arange(length), order] = 1.0
    picks = np.stack([pick, pick.T]).astype(jnp.bfloat16)
    return np.concatenate([high, low, picks], axis=0)


def parts_of(value):
    high = value.astype(jnp.bfloat16)
    low = (value - high.astype(jnp.float32)).astype(jnp.bfloat16)
    return high, low


def dot(a, b):
    return jnp.dot(a, b, preferred_element_type=jnp.float32)


def scratch_list(depth_count, stripe_count, capacity, length, width, tables):
    dma, regular = pltpu.SemaphoreType.DMA, pltpu.SemaphoreType.REGULAR
    chunk = length // CHUNKS
    count = tables // 4
    field = (2, length, length)
    items = [
        ("obj", pltpu.VMEM((2, length, width), jnp.float32)),
        ("stage", pltpu.VMEM((2, length, width), jnp.int16)),
        ("win", pltpu.VMEM((capacity, length, length), jnp.int16)),
        ("wins", pltpu.VMEM((depth_count,) + field, jnp.int16)),
        ("waves", pltpu.VMEM((depth_count,) + field, jnp.float32)),
        ("gout", pltpu.VMEM((depth_count,) + field, jnp.int16)),
        ("gscale", pltpu.VMEM((depth_count, 2, CHUNKS, 1, length), jnp.float32)),
        ("gin", pltpu.VMEM((capacity, length, length), jnp.int16)),
        ("gin_scale", pltpu.VMEM((capacity, CHUNKS, 1, length), jnp.float32)),
        ("rstack", pltpu.VMEM((count, 3 * length, length), jnp.bfloat16)),
        ("lstack", pltpu.VMEM((count, length, 3 * length), jnp.bfloat16)),
        ("picks", pltpu.VMEM((2, length, length), jnp.bfloat16)),
        ("probe", pltpu.VMEM(field, jnp.bfloat16)),
        ("amp", pltpu.VMEM((capacity, length, length), jnp.bfloat16)),
        ("amp_send", pltpu.VMEM((2, length, length), jnp.bfloat16)),
        ("patterns", pltpu.VMEM((stripe_count, length, length), jnp.bfloat16)),
        ("adj", pltpu.VMEM(field, jnp.float32)),
        ("far", pltpu.VMEM((2, length, width), jnp.int16)),
        ("far_scale", pltpu.VMEM((2, CHUNKS, 1, width), jnp.float32)),
        ("given", pltpu.VMEM((2, length, width), jnp.int16)),
        ("given_scale", pltpu.VMEM((2, CHUNKS, 1, width), jnp.float32)),
        ("own", pltpu.VMEM((length, width), jnp.float32)),
        ("mate", pltpu.VMEM((length, width), jnp.float32)),
        ("mate_in", pltpu.VMEM((length, width), jnp.float32)),
        ("out", pltpu.VMEM((2, length, width), jnp.float32)),
        ("sem_obj", dma((CHUNKS,))),
        ("sem_r", dma((count,))),
        ("sem_l", dma((count,))),
        ("sem_p", dma((3,))),
        ("sem_out", dma((CHUNKS,))),
        ("ready", regular((capacity,))),
        ("send_n", dma((3,))),
        ("recv_n", dma((CHUNKS, stripe_count))),
        ("send_w", dma((capacity,))),
        ("recv_w", dma((depth_count,))),
        ("send_a", dma((2,))),
        ("recv_a", dma((stripe_count,))),
        ("send_g", dma((depth_count, 2))),
        ("send_gs", dma((depth_count, 2))),
        ("recv_g", dma((capacity, CHUNKS))),
        ("recv_gs", dma((capacity,))),
        ("send_f", dma((2,))),
        ("send_fs", dma((2,))),
        ("recv_f", dma((2, CHUNKS))),
        ("recv_fs", dma((2, CHUNKS))),
        ("send_m", dma),
        ("recv_m", dma((CHUNKS,))),
    ]
    for k in range(CHUNKS):
        items.append((f"slab{k}", pltpu.VMEM((stripe_count, chunk, width), jnp.int16)))
    return items


def kernel(names, sizes, positions_ref, counts_ref, object_hbm, probe_hbm, amp_hbm, table_hbm, out_hbm, *scratch):
    depth_count, stripe_count, capacity, length, width = sizes
    x = types.SimpleNamespace(**dict(zip(names, scratch, strict=True)))
    slabs = [getattr(x, f"slab{k}") for k in range(CHUNKS)]
    half, chunk = length // 2, length // CHUNKS
    count = x.rstack.shape[0]
    me, stripe = lax.axis_index("depth"), lax.axis_index("stripe")
    core, side = lax.rem(stripe, 2), stripe // 2
    partner = stripe + 1 - 2 * core
    across = lax.rem(2 * side + 2, stripe_count)
    first_worker = depth_count // 2 - capacity // 2
    workers = [first_worker + j for j in range(capacity)]
    in_plane = (me >= first_worker) & (me < first_worker + capacity)
    my_j = jnp.clip(me - first_worker, 0, capacity - 1)
    is_worker = in_plane & (core == 0)
    rows_of = [pl.ds(k * chunk, chunk) for k in range(CHUNKS)]

    def remote(src, dst, send, recv, depth, where):
        return pltpu.make_async_remote_copy(
            src_ref=src, dst_ref=dst, send_sem=send, recv_sem=recv, device_id=(depth, where), device_id_type=MESH
        )

    def arrived(ref, sem):
        pltpu.make_async_copy(ref, ref, sem).wait()

    def slot_of(place):
        owner, passed, start = jnp.int32(0), jnp.int32(0), jnp.int32(0)
        for other in range(1, stripe_count):
            passed = passed + counts_ref[other - 1]
            owner = owner + jnp.where(place >= passed, 1, 0)
            start = jnp.where(place >= passed, passed, start)
        within = jnp.clip(place - start, 0, capacity - 1)
        slot = owner * capacity + within
        return owner, within, positions_ref[0, slot], positions_ref[1, slot]

    for k in range(CHUNKS):
        pltpu.make_async_copy(object_hbm.at[0, :, rows_of[k]], x.obj.at[:, rows_of[k]], x.sem_obj.at[k]).start()

    barrier = pltpu.get_barrier_semaphore()
    for step in range(1, stripe_count):
        other = lax.rem(stripe + step, stripe_count)
        pl.semaphore_signal(barrier, inc=1, device_id=(me, other), device_id_type=MESH)

    @pl.when(is_worker)
    def _():
        @pl.loop(me + 1, depth_count)
        def _(layer):
            for cc in range(2):
                pl.semaphore_signal(barrier, inc=1, device_id=(layer, 2 * side + cc), device_id_type=MESH)

    @pl.when(jnp.logical_not(is_worker))
    def _():
        for worker in workers:
            @pl.when(me < worker)
            def _():
                pl.semaphore_signal(barrier, inc=1, device_id=(worker, 2 * side), device_id_type=MESH)

    @pl.when(in_plane)
    def _():
        pltpu.make_async_copy(amp_hbm, x.amp, x.sem_p.at[0]).start()
        pltpu.make_async_copy(table_hbm.at[pl.ds(4 * count, 2)], x.picks, x.sem_p.at[1]).start()

    @pl.when(is_worker)
    def _():
        pltpu.make_async_copy(probe_hbm, x.probe, x.sem_p.at[2]).start()
        for which in range(count):
            high, low = 2 * which, 2 * count + 2 * which
            for place, source in enumerate((high, low, high)):
                span = pl.ds(place * length, length)
                pltpu.make_async_copy(table_hbm.at[source], x.rstack.at[which, span], x.sem_r.at[which]).start()
                pltpu.make_async_copy(table_hbm.at[source + 1], x.lstack.at[which, :, span], x.sem_l.at[which]).start()

    def quantize(k):
        pltpu.make_async_copy(object_hbm.at[0, :, rows_of[k]], x.obj.at[:, rows_of[k]], x.sem_obj.at[k]).wait()
        for part in range(2):
            whole = jnp.round(x.obj[part, rows_of[k]] * LEVELS).astype(jnp.int32).astype(jnp.int16)
            x.stage[part, rows_of[k]] = whole
        slabs[k][stripe] = x.stage[core, rows_of[k]]

    def spread(k):
        for cc in range(2):
            remote(
                x.stage.at[cc, rows_of[k]], slabs[k].at[stripe], x.send_n.at[cc], x.recv_n.at[k, stripe], me, across + cc
            ).start()
        remote(
            x.stage.at[1 - core, rows_of[k]], slabs[k].at[stripe], x.send_n.at[2], x.recv_n.at[k, stripe], me, partner
        ).start()

    quantize(0)
    with jax.named_scope("barrier"):
        lower_workers = jnp.clip(me - first_worker, 0, capacity)
        pl.semaphore_wait(barrier, stripe_count - 1 + jnp.where(is_worker, 2 * me, lower_workers))

    @pl.when(is_worker)
    def _():
        @pl.loop(0, me)
        def _(layer):
            for cc in range(2):
                pl.semaphore_signal(x.ready.at[my_j], inc=1, device_id=(layer, 2 * side + cc), device_id_type=MESH)

    for k in range(CHUNKS):
        if k > 0:
            quantize(k)
        spread(k)

    @pl.when(in_plane)
    def _():
        pltpu.make_async_copy(amp_hbm, x.amp, x.sem_p.at[0]).wait()
        pltpu.make_async_copy(table_hbm.at[pl.ds(4 * count, 2)], x.picks, x.sem_p.at[1]).wait()
        for target in range(2):
            _, within, _, _ = slot_of(capacity * target + my_j)
            moved = dot(x.picks[0], x.amp[within]).astype(jnp.bfloat16)
            x.amp_send[target] = dot(moved, x.picks[1]).astype(jnp.bfloat16)

            @pl.when(stripe == 2 * target)
            def _():
                pltpu.make_async_copy(x.amp_send.at[target], x.patterns.at[stripe], x.recv_a.at[stripe]).start()

            @pl.when(stripe != 2 * target)
            def _():
                remote(
                    x.amp_send.at[target], x.patterns.at[stripe], x.send_a.at[target], x.recv_a.at[stripe], me, 2 * target
                ).start()

    my_owner, _, my_row, my_col = slot_of(capacity * side + my_j)

    @pl.when(is_worker)
    def _():
        pltpu.make_async_copy(probe_hbm, x.probe, x.sem_p.at[2]).wait()
        first = lax.broadcasted_iota(jnp.int32, (length, length), 0)
        second = lax.broadcasted_iota(jnp.int32, (length, length), 1)
        turned = second + my_row
        turned = jnp.where(turned >= length, turned - length, turned)
        turn_rows = jnp.where(first == turned, 1.0, 0.0).astype(jnp.bfloat16)
        turned = first + my_col
        turned = jnp.where(turned >= length, turned - length, turned)
        turn_cols = jnp.where(second == turned, 1.0, 0.0).astype(jnp.bfloat16)
        for part in range(2):
            value = dot(turn_rows, x.probe[part]).astype(jnp.bfloat16)
            x.waves[0, part] = dot(value, turn_cols)

    row_index = lax.broadcasted_iota(jnp.int32, (chunk, half), 0)
    col_index = lax.broadcasted_iota(jnp.int32, (chunk, half), 1)

    def each_worker(action):
        for j, worker in enumerate(workers):
            here = (me == worker) & (core == 0)
            action(j, worker, here)

    def cut(k):
        for step in range(1, stripe_count):
            other = lax.rem(stripe + step, stripe_count)
            arrived(slabs[k].at[other], x.recv_n.at[k, other])
        for j, worker in enumerate(workers):
            owner, _, row, col = slot_of(capacity * side + j)
            later = lax.rem(owner + 1, stripe_count)
            here = row_index >= row - k * chunk
            near = col_index >= col
            left, mid, right = (
                jnp.where(
                    here,
                    slabs[k][owner, :, pl.ds(place * half, half)].astype(jnp.int32),
                    slabs[k][later, :, pl.ds(place * half, half)].astype(jnp.int32),
                )
                for place in range(3)
            )
            x.win[j, rows_of[k], pl.ds(0, half)] = jnp.where(near, left, right).astype(jnp.int16)
            x.win[j, rows_of[k], pl.ds(half, half)] = mid.astype(jnp.int16)

            local = (me == worker) & (core == 0)
            if k == 0:
                @pl.when(me < worker)
                def _():
                    pl.semaphore_wait(x.ready.at[j], 1)

            source, target = x.win.at[j, rows_of[k]], x.wins.at[me, core, rows_of[k]]

            @pl.when(jnp.logical_not(local))
            def _():
                remote(source, target, x.send_w.at[j], x.recv_w.at[me], worker, 2 * side).start()

            @pl.when(local)
            def _():
                pltpu.make_async_copy(source, target, x.recv_w.at[me]).start()

    for k in range(CHUNKS):
        with jax.named_scope(f"cut{k}"):
            cut(k)

    def right_dot(value, which):
        high, low = parts_of(value)
        return dot(jnp.concatenate([high, high, low], axis=1), x.rstack[which])

    def left_dot(which, value):
        high, low = parts_of(value)
        return dot(x.lstack[which], jnp.concatenate([high, high, low], axis=0))

    def split_lanes(re, im):
        return (
            jnp.concatenate([re[:, :half] + re[:, half:], im[:, :half] + im[:, half:]], axis=1),
            jnp.concatenate([re[:, :half] - re[:, half:], im[:, :half] - im[:, half:]], axis=1),
        )

    def split_rows(re, im):
        return (
            jnp.concatenate([re[:half] + re[half:], im[:half] + im[half:]], axis=0),
            jnp.concatenate([re[:half] - re[half:], im[:half] - im[half:]], axis=0),
        )

    def join_lanes(p, q):
        return (
            jnp.concatenate([p[:, :half] + q[:, :half], p[:, :half] - q[:, :half]], axis=1),
            jnp.concatenate([p[:, half:] + q[:, half:], p[:, half:] - q[:, half:]], axis=1),
        )

    def join_rows(p, q):
        return (
            jnp.concatenate([p[:half] + q[:half], p[:half] - q[:half]], axis=0),
            jnp.concatenate([p[half:] + q[half:], p[half:] - q[half:]], axis=0),
        )

    def propagate(re, im):
        u, v = split_lanes(re, im)
        re, im = join_lanes(right_dot(u, 0), right_dot(v, 1))
        u, v = split_rows(re, im)
        return join_rows(left_dot(0, u), left_dot(1, v))

    def window_of(layer):
        value = x.wins[layer].astype(jnp.int32).astype(jnp.float32) * (1.0 / LEVELS)
        return value[0], value[1]

    def emit(layer, re, im):
        for part, value in enumerate((re, im)):
            for k in range(CHUNKS):
                piece = value[k * chunk : (k + 1) * chunk]
                most = jnp.maximum(jnp.max(jnp.abs(piece), axis=0, keepdims=True), 1e-30)
                x.gout[layer, part, rows_of[k]] = jnp.round(piece * (LEVELS / most)).astype(jnp.int32).astype(jnp.int16)
                x.gscale[layer, part, k] = most * (1.0 / LEVELS)

        def scale_copy(part):
            return remote(
                x.gscale.at[layer, part], x.gin_scale.at[my_j], x.send_gs.at[layer, part], x.recv_gs.at[my_j], layer,
                2 * side + part,
            )

        def chunk_copy(part, k):
            return remote(
                x.gout.at[layer, part, rows_of[k]], x.gin.at[my_j, rows_of[k]], x.send_g.at[layer, part],
                x.recv_g.at[my_j, k], layer, 2 * side + part,
            )

        @pl.when(layer != me)
        def _():
            scale_copy(0).start()

        @pl.when(layer == me)
        def _():
            pltpu.make_async_copy(x.gscale.at[layer, 0], x.gin_scale.at[my_j], x.recv_gs.at[my_j]).start()

        scale_copy(1).start()
        for k in range(CHUNKS):
            @pl.when(layer != me)
            def _():
                chunk_copy(0, k).start()

            @pl.when(layer == me)
            def _():
                pltpu.make_async_copy(
                    x.gout.at[layer, 0, rows_of[k]], x.gin.at[my_j, rows_of[k]], x.recv_g.at[my_j, k]
                ).start()

            chunk_copy(1, k).start()

    @pl.when(is_worker)
    def _():
        for which in range(count):
            arrived(x.rstack.at[which], x.sem_r.at[which])
            arrived(x.lstack.at[which], x.sem_l.at[which])

        @pl.loop(0, depth_count - 1)
        def forward(layer):
            with jax.named_scope("fw_wait"):
                arrived(x.wins.at[layer], x.recv_w.at[layer])
            win_re, win_im = window_of(layer)
            re, im = x.waves[layer, 0], x.waves[layer, 1]
            re, im = propagate(re * win_re - im * win_im, re * win_im + im * win_re)
            x.waves[layer + 1, 0] = re
            x.waves[layer + 1, 1] = im

        last = depth_count - 1
        with jax.named_scope("last_wait"):
            arrived(x.wins.at[last], x.recv_w.at[last])
        win_re, win_im = window_of(last)
        wave_re, wave_im = x.waves[last, 0], x.waves[last, 1]
        re = wave_re * win_re - wave_im * win_im
        im = wave_re * win_im + wave_im * win_re
        u, v = split_lanes(re, im)
        even, odd = right_dot(u, 2), right_dot(v, 3)
        re = jnp.concatenate([even[:, :half], odd[:, :half]], axis=1)
        im = jnp.concatenate([even[:, half:], odd[:, half:]], axis=1)
        u, v = split_rows(re, im)
        even, odd = left_dot(2, u), left_dot(3, v)
        with jax.named_scope("amp_wait"):
            for source in range(stripe_count):
                arrived(x.patterns.at[source], x.recv_a.at[source])
        amp = x.patterns[my_owner].astype(jnp.float32)
        re = jnp.concatenate([even[:half], odd[:half]], axis=0)
        im = jnp.concatenate([even[half:], odd[half:]], axis=0)
        factor = 1.0 - amp / jnp.sqrt(re * re + im * im + smoothing)
        re, im = factor * re, factor * im

        def left_back(which, value):
            high, low = parts_of(value)
            table = x.rstack[which, pl.ds(0, length)]
            table_low = x.rstack[which, pl.ds(length, length)]
            return dot(table, high) + dot(table_low, high) + dot(table, low)

        def right_back(value, which):
            high, low = parts_of(value)
            table = x.lstack[which, :, pl.ds(0, length)]
            table_low = x.lstack[which, :, pl.ds(length, length)]
            return dot(high, table) + dot(high, table_low) + dot(low, table)

        re, im = join_rows(
            left_back(2, jnp.concatenate([re[:half], im[:half]], axis=0)),
            left_back(3, jnp.concatenate([re[half:], im[half:]], axis=0)),
        )
        mid_re, mid_im = join_lanes(
            right_back(jnp.concatenate([re[:, :half], im[:, :half]], axis=1), 2),
            right_back(jnp.concatenate([re[:, half:], im[:, half:]], axis=1), 3),
        )
        emit(
            last,
            wave_re * mid_re + wave_im * mid_im,
            wave_re * mid_im - wave_im * mid_re,
        )
        x.adj[0] = win_re * mid_re + win_im * mid_im
        x.adj[1] = win_im * mid_re - win_re * mid_im

        @pl.loop(1, depth_count)
        def backward(step):
            layer = last - step
            with jax.named_scope("bw"):
                mid_re, mid_conj = propagate(x.adj[0], x.adj[1])
                win_re, win_im = window_of(layer)
                wave_re, wave_im = x.waves[layer, 0], x.waves[layer, 1]
                emit(
                    layer,
                    wave_re * mid_re - wave_im * mid_conj,
                    -(wave_re * mid_conj + wave_im * mid_re),
                )
                x.adj[0] = win_re * mid_re - win_im * mid_conj
                x.adj[1] = win_im * mid_re + win_re * mid_conj

    def far_copy(cc, k):
        return remote(
            x.far.at[cc, rows_of[k]], x.given.at[core, rows_of[k]], x.send_f.at[cc], x.recv_f.at[core, k], me, across + cc
        )

    def far_scale_copy(cc, k):
        return remote(
            x.far_scale.at[cc, k], x.given_scale.at[core, k], x.send_fs.at[cc], x.recv_fs.at[core, k], me, across + cc
        )

    def mate_copy(k):
        return remote(x.mate.at[rows_of[k]], x.mate_in.at[rows_of[k]], x.send_m, x.recv_m.at[k], me, partner)

    def out_copy(k):
        return pltpu.make_async_copy(x.out.at[:, rows_of[k]], out_hbm.at[0, :, rows_of[k]], x.sem_out.at[k])

    def reduce_chunk(k):
        with jax.named_scope(f"gin_wait{k}"):
            for j in range(capacity):
                if k == 0:
                    arrived(x.gin_scale.at[j], x.recv_gs.at[j])
                arrived(x.gin.at[j, rows_of[k]], x.recv_g.at[j, k])
        targets = [stripe, partner, across, across + 1]
        sums = [[0.0] * 3 for _ in targets]
        for j in range(capacity):
            owner, _, row, col = slot_of(capacity * side + j)
            later = lax.rem(owner + 1, stripe_count)
            here = row_index >= row - k * chunk
            near = col_index >= col
            scale = x.gin_scale[j, k]
            left = x.gin[j, rows_of[k], pl.ds(0, half)].astype(jnp.int32).astype(jnp.float32) * scale[:, :half]
            mid = x.gin[j, rows_of[k], pl.ds(half, half)].astype(jnp.int32).astype(jnp.float32) * scale[:, half:]
            pieces = (jnp.where(near, left, 0.0), mid, jnp.where(near, 0.0, left))
            for t, target in enumerate(targets):
                gain = jnp.where(
                    here, jnp.where(owner == target, 1.0, 0.0), jnp.where(later == target, 1.0, 0.0)
                )
                for place, piece in enumerate(pieces):
                    sums[t][place] = sums[t][place] + piece * gain
        for cc in range(2):
            for place in range(3):
                lanes = pl.ds(place * half, half)
                total = sums[2 + cc][place]
                most = jnp.maximum(jnp.max(jnp.abs(total), axis=0, keepdims=True), 1e-30)
                x.far[cc, rows_of[k], lanes] = jnp.round(total * (LEVELS / most)).astype(jnp.int32).astype(jnp.int16)
                x.far_scale[cc, k, :, lanes] = most * (1.0 / LEVELS)
            far_copy(cc, k).start()
            far_scale_copy(cc, k).start()
        for place in range(3):
            lanes = pl.ds(place * half, half)
            x.mate[rows_of[k], lanes] = sums[1][place]
            x.own[rows_of[k], lanes] = sums[0][place]
        mate_copy(k).start()

    def finish_chunk(k):
        with jax.named_scope(f"far_wait{k}"):
            for part in range(2):
                arrived(x.given.at[part, rows_of[k]], x.recv_f.at[part, k])
                arrived(x.given_scale.at[part, k], x.recv_fs.at[part, k])
            arrived(x.mate_in.at[rows_of[k]], x.recv_m.at[k])
        for part, base in ((core, x.own), (1 - core, x.mate_in)):
            value = x.given[part, rows_of[k]].astype(jnp.int32).astype(jnp.float32)
            x.out[part, rows_of[k]] = base[rows_of[k]] + value * x.given_scale[part, k]
        out_copy(k).start()

    for k in range(CHUNKS):
        reduce_chunk(k)
        if k > 0:
            finish_chunk(k - 1)
    finish_chunk(CHUNKS - 1)

    for k in range(CHUNKS):
        out_copy(k).wait()
    for cc in range(2):
        arrived(x.stage.at[cc], x.send_n.at[cc])
        arrived(x.far.at[cc], x.send_f.at[cc])
        arrived(x.far_scale.at[cc], x.send_fs.at[cc])
    arrived(x.stage.at[0], x.send_n.at[2])
    arrived(x.mate, x.send_m)
    for j, worker in enumerate(workers):
        @pl.when(jnp.logical_not((me == worker) & (core == 0)))
        def _():
            arrived(x.win.at[j], x.send_w.at[j])

    @pl.when(in_plane)
    def _():
        for target in range(2):
            @pl.when(stripe != 2 * target)
            def _():
                arrived(x.amp_send.at[target], x.send_a.at[target])

    @pl.when(is_worker)
    def _():
        @pl.loop(0, depth_count)
        def _(layer):
            arrived(x.gout.at[layer, 1], x.send_g.at[layer, 1])
            arrived(x.gscale.at[layer, 1], x.send_gs.at[layer, 1])

            @pl.when(layer != me)
            def _():
                arrived(x.gout.at[layer, 0], x.send_g.at[layer, 0])
                arrived(x.gscale.at[layer, 0], x.send_gs.at[layer, 0])


def body(tables, object_slices, probe_wave, amplitudes, positions, counts):
    stripe_count = lax.axis_size("stripe")
    depth_count = lax.axis_size("depth")
    layers, _, stripe_rows, width = object_slices.shape
    length = probe_wave.shape[1]
    capacity = amplitudes.shape[0]
    assert layers == 1 and stripe_rows == length and 2 * width == 3 * length
    assert depth_count >= capacity and stripe_count == 4
    items = scratch_list(depth_count, stripe_count, capacity, length, width, tables.shape[0] - 2)
    smem = pl.BlockSpec(memory_space=pltpu.SMEM)
    sizes = (depth_count, stripe_count, capacity, length, width)
    return pl.pallas_call(
        functools.partial(kernel, [name for name, _ in items], sizes),
        out_shape=jax.ShapeDtypeStruct(object_slices.shape, jnp.float32),
        in_specs=[smem] * 2 + [pl.BlockSpec(memory_space=pl.ANY)] * 4,
        out_specs=pl.BlockSpec(memory_space=pl.ANY),
        scratch_shapes=[shape for _, shape in items],
        compiler_params=pltpu.CompilerParams(
            collective_id=0, has_side_effects=True, vmem_limit_bytes=60 * 1024 * 1024
        ),
    )(positions.T, counts, object_slices, probe_wave, amplitudes, tables)


def solution(mesh):
    def run(object_slices, probe_wave, amplitudes, positions, counts):
        tables = jnp.asarray(make_tables(probe_wave.shape[1]))
        return jax.shard_map(
            body,
            mesh=mesh,
            in_specs=(P(), P("depth", None, "stripe", None), P(), P("stripe", None, None), P(), P()),
            out_specs=P("depth", None, "stripe", None),
            check_vma=False,
        )(tables, object_slices, probe_wave, amplitudes, positions, counts)

    return run
```

time: 71.6 us -> 61.1 us (0.85)
  Pallas kernels: 69.3 us -> 58.8 us
    pallas_call x1, Pallas kernels: 69.3 us -> 58.8 us  [body(): pl.pallas_call(functools.partial(kernel, [name for name, _ in items], siz...]
where the time goes in v1:
time: 61.1 us; the launch traced here: 60.9 us
  Pallas kernels  58.8 us (96%)
  local copies, waits for them, and re-layouts  2.06 us (3%)
    pallas_call x1, Pallas kernels, body(): pl.pallas_call(functools.partial(kernel, [name for name, _ in items], siz...  58.8 us
    unnamed x1, local copies, waits for them, and re-layouts  2.06 us

profile of v1, /device:TPU:1, one launch (start us, length us, event | category | flops | bytes accessed | tf_op | source)
XLA Modules:
  0.0 60.9 jit_solution(8570090205205444658)
XLA Ops:
  0.0 58.8 %shard_map.64 = f32[1,2,256,384]{3,2,1,0:T(8,128)} custom-call(s32[2,16]{1,0:T(2,128)} %bitcast.1, s32[4]{0:T(128)} %counts_ref.1, f32[1,2,256,384]{3,2,1,0:T(8,128)} %object_hbm.1, bf16[2,256,256]{2,1,0:T(8,128)(2,1)} %probe_hbm.1, bf16[4,256,256]{2,1,0:T(8,128)(2,1)} %amp_hbm.1, bf16[18,256,256]{2,1,0:T(8,128)(2,1)} %constant.2.clone.table_hbm), custom_call_target="tpu_custom_call" | custom-call | tf_op jit(solution)/shard_map/pallas_call | solution.py:583
  58.8 2.1 %copy.8 = f32[1,2,256,384]{3,2,1,0:T(8,128)} copy(f32[1,2,256,384]{3,2,1,0:T(8,128)} %shard_map.64) | data formatting | bytes 1572864

commit v2 on v1

--- a/solution.py
+++ b/solution.py
@@ -11,7 +11,10 @@
 
 smoothing = 0.25
 LEVELS = 32767.0
-CHUNKS = 4
+IN_CUTS = (32, 64, 80, 80)
+OUT_CUTS = (64, 64, 64, 64)
+LATE = 4
+ORDER = (2, 3, 1, 0)
 MESH = pl.DeviceIdType.MESH
 
 
@@ -42,6 +45,16 @@
     return np.concatenate([high, low, picks], axis=0)
 
 
+def cut_rows(length, cuts):
+    unit = length // sum(cuts)
+    sizes = [size * unit for size in cuts]
+    return [(sum(sizes[:k]), size) for k, size in enumerate(sizes)]
+
+
+def worker_depths(depth_count):
+    return [depth_count // 8, depth_count // 4, depth_count // 2, depth_count // 2 + 1]
+
+
 def parts_of(value):
     high = value.astype(jnp.bfloat16)
     low = (value - high.astype(jnp.float32)).astype(jnp.bfloat16)
@@ -54,8 +67,8 @@
 
 def scratch_list(depth_count, stripe_count, capacity, length, width, tables):
     dma, regular = pltpu.SemaphoreType.DMA, pltpu.SemaphoreType.REGULAR
-    chunk = length // CHUNKS
     count = tables // 4
+    ins, outs = len(IN_CUTS), len(OUT_CUTS)
     field = (2, length, length)
     items = [
         ("obj", pltpu.VMEM((2, length, width), jnp.float32)),
@@ -64,9 +77,9 @@
         ("wins", pltpu.VMEM((depth_count,) + field, jnp.int16)),
         ("waves", pltpu.VMEM((depth_count,) + field, jnp.float32)),
         ("gout", pltpu.VMEM((depth_count,) + field, jnp.int16)),
-        ("gscale", pltpu.VMEM((depth_count, 2, CHUNKS, 1, length), jnp.float32)),
+        ("gscale", pltpu.VMEM((depth_count, 2, outs, 1, length), jnp.float32)),
         ("gin", pltpu.VMEM((capacity, length, length), jnp.int16)),
-        ("gin_scale", pltpu.VMEM((capacity, CHUNKS, 1, length), jnp.float32)),
+        ("gin_scale", pltpu.VMEM((capacity, outs, 1, length), jnp.float32)),
         ("rstack", pltpu.VMEM((count, 3 * length, length), jnp.bfloat16)),
         ("lstack", pltpu.VMEM((count, length, 3 * length), jnp.bfloat16)),
         ("picks", pltpu.VMEM((2, length, length), jnp.bfloat16)),
@@ -76,57 +89,60 @@
         ("patterns", pltpu.VMEM((stripe_count, length, length), jnp.bfloat16)),
         ("adj", pltpu.VMEM(field, jnp.float32)),
         ("far", pltpu.VMEM((2, length, width), jnp.int16)),
-        ("far_scale", pltpu.VMEM((2, CHUNKS, 1, width), jnp.float32)),
+        ("far_scale", pltpu.VMEM((2, outs, 1, width), jnp.float32)),
         ("given", pltpu.VMEM((2, length, width), jnp.int16)),
-        ("given_scale", pltpu.VMEM((2, CHUNKS, 1, width), jnp.float32)),
+        ("given_scale", pltpu.VMEM((2, outs, 1, width), jnp.float32)),
         ("own", pltpu.VMEM((length, width), jnp.float32)),
         ("mate", pltpu.VMEM((length, width), jnp.float32)),
         ("mate_in", pltpu.VMEM((length, width), jnp.float32)),
-        ("out", pltpu.VMEM((2, length, width), jnp.float32)),
-        ("sem_obj", dma((CHUNKS,))),
+        ("positions", pltpu.SMEM((2, stripe_count * capacity), jnp.int32)),
+        ("counts", pltpu.SMEM((stripe_count,), jnp.int32)),
+        ("sem_s", dma((2,))),
+        ("sem_obj", dma((ins,))),
         ("sem_r", dma((count,))),
         ("sem_l", dma((count,))),
         ("sem_p", dma((3,))),
-        ("sem_out", dma((CHUNKS,))),
         ("ready", regular((capacity,))),
         ("send_n", dma((3,))),
-        ("recv_n", dma((CHUNKS, stripe_count))),
+        ("recv_n", dma((ins, stripe_count))),
         ("send_w", dma((capacity,))),
         ("recv_w", dma((depth_count,))),
         ("send_a", dma((2,))),
         ("recv_a", dma((stripe_count,))),
         ("send_g", dma((depth_count, 2))),
         ("send_gs", dma((depth_count, 2))),
-        ("recv_g", dma((capacity, CHUNKS))),
+        ("recv_g", dma((capacity, outs))),
         ("recv_gs", dma((capacity,))),
         ("send_f", dma((2,))),
         ("send_fs", dma((2,))),
-        ("recv_f", dma((2, CHUNKS))),
-        ("recv_fs", dma((2, CHUNKS))),
+        ("recv_f", dma((2, outs))),
+        ("recv_fs", dma((2, outs))),
         ("send_m", dma),
-        ("recv_m", dma((CHUNKS,))),
+        ("recv_m", dma((outs,))),
     ]
-    for k in range(CHUNKS):
-        items.append((f"slab{k}", pltpu.VMEM((stripe_count, chunk, width), jnp.int16)))
+    for k, (_, size) in enumerate(cut_rows(length, IN_CUTS)):
+        items.append((f"slab{k}", pltpu.VMEM((stripe_count, size, width), jnp.int16)))
     return items
 
 
-def kernel(names, sizes, positions_ref, counts_ref, object_hbm, probe_hbm, amp_hbm, table_hbm, out_hbm, *scratch):
+def kernel(names, sizes, positions_hbm, counts_hbm, object_hbm, probe_hbm, amp_hbm, table_hbm, out_ref, *scratch):
     depth_count, stripe_count, capacity, length, width = sizes
     x = types.SimpleNamespace(**dict(zip(names, scratch, strict=True)))
-    slabs = [getattr(x, f"slab{k}") for k in range(CHUNKS)]
-    half, chunk = length // 2, length // CHUNKS
+    in_cuts, out_cuts = cut_rows(length, IN_CUTS), cut_rows(length, OUT_CUTS)
+    ins, outs = len(in_cuts), len(out_cuts)
+    in_rows = [pl.ds(start, size) for start, size in in_cuts]
+    out_rows = [pl.ds(start, size) for start, size in out_cuts]
+    slabs = [getattr(x, f"slab{k}") for k in range(ins)]
+    half = length // 2
     count = x.rstack.shape[0]
     me, stripe = lax.axis_index("depth"), lax.axis_index("stripe")
     core, side = lax.rem(stripe, 2), stripe // 2
     partner = stripe + 1 - 2 * core
     across = lax.rem(2 * side + 2, stripe_count)
-    first_worker = depth_count // 2 - capacity // 2
-    workers = [first_worker + j for j in range(capacity)]
-    in_plane = (me >= first_worker) & (me < first_worker + capacity)
-    my_j = jnp.clip(me - first_worker, 0, capacity - 1)
+    workers = worker_depths(depth_count)
+    in_plane = functools.reduce(jnp.logical_or, [me == worker for worker in workers])
+    my_j = sum(jnp.where(me == worker, j, 0) for j, worker in enumerate(workers))
     is_worker = in_plane & (core == 0)
-    rows_of = [pl.ds(k * chunk, chunk) for k in range(CHUNKS)]
 
     def remote(src, dst, send, recv, depth, where):
         return pltpu.make_async_remote_copy(
@@ -139,15 +155,24 @@
     def slot_of(place):
         owner, passed, start = jnp.int32(0), jnp.int32(0), jnp.int32(0)
         for other in range(1, stripe_count):
-            passed = passed + counts_ref[other - 1]
+            passed = passed + x.counts[other - 1]
             owner = owner + jnp.where(place >= passed, 1, 0)
             start = jnp.where(place >= passed, passed, start)
         within = jnp.clip(place - start, 0, capacity - 1)
         slot = owner * capacity + within
-        return owner, within, positions_ref[0, slot], positions_ref[1, slot]
-
-    for k in range(CHUNKS):
-        pltpu.make_async_copy(object_hbm.at[0, :, rows_of[k]], x.obj.at[:, rows_of[k]], x.sem_obj.at[k]).start()
+        return owner, within, x.positions[0, slot], x.positions[1, slot]
+
+    def scalar_loads():
+        return [
+            pltpu.make_async_copy(positions_hbm, x.positions, x.sem_s.at[0]),
+            pltpu.make_async_copy(counts_hbm, x.counts, x.sem_s.at[1]),
+        ]
+
+    for k in range(ins):
+        pltpu.make_async_copy(object_hbm.at[0, :, in_rows[k]], x.obj.at[:, in_rows[k]], x.sem_obj.at[k]).start()
+
+    for copy in scalar_loads():
+        copy.start()
 
     barrier = pltpu.get_barrier_semaphore()
     for step in range(1, stripe_count):
@@ -184,24 +209,24 @@
                 pltpu.make_async_copy(table_hbm.at[source + 1], x.lstack.at[which, :, span], x.sem_l.at[which]).start()
 
     def quantize(k):
-        pltpu.make_async_copy(object_hbm.at[0, :, rows_of[k]], x.obj.at[:, rows_of[k]], x.sem_obj.at[k]).wait()
+        pltpu.make_async_copy(object_hbm.at[0, :, in_rows[k]], x.obj.at[:, in_rows[k]], x.sem_obj.at[k]).wait()
         for part in range(2):
-            whole = jnp.round(x.obj[part, rows_of[k]] * LEVELS).astype(jnp.int32).astype(jnp.int16)
-            x.stage[part, rows_of[k]] = whole
-        slabs[k][stripe] = x.stage[core, rows_of[k]]
+            whole = jnp.round(x.obj[part, in_rows[k]] * LEVELS).astype(jnp.int32).astype(jnp.int16)
+            x.stage[part, in_rows[k]] = whole
+        slabs[k][stripe] = x.stage[core, in_rows[k]]
 
     def spread(k):
         for cc in range(2):
             remote(
-                x.stage.at[cc, rows_of[k]], slabs[k].at[stripe], x.send_n.at[cc], x.recv_n.at[k, stripe], me, across + cc
+                x.stage.at[cc, in_rows[k]], slabs[k].at[stripe], x.send_n.at[cc], x.recv_n.at[k, stripe], me, across + cc
             ).start()
         remote(
-            x.stage.at[1 - core, rows_of[k]], slabs[k].at[stripe], x.send_n.at[2], x.recv_n.at[k, stripe], me, partner
+            x.stage.at[1 - core, in_rows[k]], slabs[k].at[stripe], x.send_n.at[2], x.recv_n.at[k, stripe], me, partner
         ).start()
 
     quantize(0)
     with jax.named_scope("barrier"):
-        lower_workers = jnp.clip(me - first_worker, 0, capacity)
+        lower_workers = sum(jnp.where(worker < me, 1, 0) for worker in workers)
         pl.semaphore_wait(barrier, stripe_count - 1 + jnp.where(is_worker, 2 * me, lower_workers))
 
     @pl.when(is_worker)
@@ -211,10 +236,13 @@
             for cc in range(2):
                 pl.semaphore_signal(x.ready.at[my_j], inc=1, device_id=(layer, 2 * side + cc), device_id_type=MESH)
 
-    for k in range(CHUNKS):
+    for k in range(ins):
         if k > 0:
             quantize(k)
         spread(k)
+
+    for copy in scalar_loads():
+        copy.wait()
 
     @pl.when(in_plane)
     def _():
@@ -252,23 +280,38 @@
             value = dot(turn_rows, x.probe[part]).astype(jnp.bfloat16)
             x.waves[0, part] = dot(value, turn_cols)
 
-    row_index = lax.broadcasted_iota(jnp.int32, (chunk, half), 0)
-    col_index = lax.broadcasted_iota(jnp.int32, (chunk, half), 1)
-
-    def each_worker(action):
-        for j, worker in enumerate(workers):
-            here = (me == worker) & (core == 0)
-            action(j, worker, here)
+    def rows_from(size):
+        return lax.broadcasted_iota(jnp.int32, (size, half), 0)
+
+    def cols_from(size):
+        return lax.broadcasted_iota(jnp.int32, (size, half), 1)
+
+    order = ORDER
+
+    def local(j):
+        return (me == workers[j]) & (core == 0)
+
+    def window_send(j, rows):
+        source, target = x.win.at[j, rows], x.wins.at[me, core, rows]
+
+        @pl.when(jnp.logical_not(local(j)))
+        def _():
+            remote(source, target, x.send_w.at[j], x.recv_w.at[me], workers[j], 2 * side).start()
+
+        @pl.when(local(j))
+        def _():
+            pltpu.make_async_copy(source, target, x.recv_w.at[me]).start()
 
     def cut(k):
         for step in range(1, stripe_count):
             other = lax.rem(stripe + step, stripe_count)
             arrived(slabs[k].at[other], x.recv_n.at[k, other])
-        for j, worker in enumerate(workers):
+        start, size = in_cuts[k]
+        for j in order:
             owner, _, row, col = slot_of(capacity * side + j)
             later = lax.rem(owner + 1, stripe_count)
-            here = row_index >= row - k * chunk
-            near = col_index >= col
+            here = rows_from(size) >= row - start
+            near = cols_from(size) >= col
             left, mid, right = (
                 jnp.where(
                     here,
@@ -277,28 +320,19 @@
                 )
                 for place in range(3)
             )
-            x.win[j, rows_of[k], pl.ds(0, half)] = jnp.where(near, left, right).astype(jnp.int16)
-            x.win[j, rows_of[k], pl.ds(half, half)] = mid.astype(jnp.int16)
-
-            local = (me == worker) & (core == 0)
+            x.win[j, in_rows[k], pl.ds(0, half)] = jnp.where(near, left, right).astype(jnp.int16)
+            x.win[j, in_rows[k], pl.ds(half, half)] = mid.astype(jnp.int16)
+
             if k == 0:
-                @pl.when(me < worker)
+                @pl.when(me < workers[j])
                 def _():
                     pl.semaphore_wait(x.ready.at[j], 1)
 
-            source, target = x.win.at[j, rows_of[k]], x.wins.at[me, core, rows_of[k]]
-
-            @pl.when(jnp.logical_not(local))
-            def _():
-                remote(source, target, x.send_w.at[j], x.recv_w.at[me], worker, 2 * side).start()
-
-            @pl.when(local)
-            def _():
-                pltpu.make_async_copy(source, target, x.recv_w.at[me]).start()
-
-    for k in range(CHUNKS):
+    for k in range(ins):
         with jax.named_scope(f"cut{k}"):
             cut(k)
+        for j in order:
+            window_send(j, in_rows[k])
 
     def right_dot(value, which):
         high, low = parts_of(value)
@@ -342,12 +376,32 @@
         value = x.wins[layer].astype(jnp.int32).astype(jnp.float32) * (1.0 / LEVELS)
         return value[0], value[1]
 
+    def gradient_copies(layer, k, action):
+        for part in range(2):
+            @pl.when((layer != me) | (part == 1))
+            def _():
+                action(
+                    remote(
+                        x.gout.at[layer, part, out_rows[k]], x.gin.at[my_j, out_rows[k]], x.send_g.at[layer, part],
+                        x.recv_g.at[my_j, k], layer, 2 * side + part,
+                    )
+                )
+
+        @pl.when(layer == me)
+        def _():
+            action(
+                pltpu.make_async_copy(
+                    x.gout.at[layer, 0, out_rows[k]], x.gin.at[my_j, out_rows[k]], x.recv_g.at[my_j, k]
+                )
+            )
+
     def emit(layer, re, im):
         for part, value in enumerate((re, im)):
-            for k in range(CHUNKS):
-                piece = value[k * chunk : (k + 1) * chunk]
+            for k in range(outs):
+                start, size = out_cuts[k]
+                piece = value[start : start + size]
                 most = jnp.maximum(jnp.max(jnp.abs(piece), axis=0, keepdims=True), 1e-30)
-                x.gout[layer, part, rows_of[k]] = jnp.round(piece * (LEVELS / most)).astype(jnp.int32).astype(jnp.int16)
+                x.gout[layer, part, out_rows[k]] = jnp.round(piece * (LEVELS / most)).astype(jnp.int32).astype(jnp.int16)
                 x.gscale[layer, part, k] = most * (1.0 / LEVELS)
 
         def scale_copy(part):
@@ -356,12 +410,6 @@
                 2 * side + part,
             )
 
-        def chunk_copy(part, k):
-            return remote(
-                x.gout.at[layer, part, rows_of[k]], x.gin.at[my_j, rows_of[k]], x.send_g.at[layer, part],
-                x.recv_g.at[my_j, k], layer, 2 * side + part,
-            )
-
         @pl.when(layer != me)
         def _():
             scale_copy(0).start()
@@ -371,18 +419,12 @@
             pltpu.make_async_copy(x.gscale.at[layer, 0], x.gin_scale.at[my_j], x.recv_gs.at[my_j]).start()
 
         scale_copy(1).start()
-        for k in range(CHUNKS):
-            @pl.when(layer != me)
+        for k in range(outs):
+            held = layer + k
+
+            @pl.when((held < depth_count) & ((held >= LATE) | (k == 0)))
             def _():
-                chunk_copy(0, k).start()
-
-            @pl.when(layer == me)
-            def _():
-                pltpu.make_async_copy(
-                    x.gout.at[layer, 0, rows_of[k]], x.gin.at[my_j, rows_of[k]], x.recv_g.at[my_j, k]
-                ).start()
-
-            chunk_copy(1, k).start()
+                gradient_copies(held, k, lambda copy: copy.start())
 
     @pl.when(is_worker)
     def _():
@@ -465,9 +507,13 @@
                 x.adj[0] = win_re * mid_re - win_im * mid_conj
                 x.adj[1] = win_im * mid_re + win_re * mid_conj
 
+        for k in range(1, outs):
+            for layer in range(LATE):
+                gradient_copies(layer, k, lambda copy: copy.start())
+
     def far_copy(cc, k):
         return remote(
-            x.far.at[cc, rows_of[k]], x.given.at[core, rows_of[k]], x.send_f.at[cc], x.recv_f.at[core, k], me, across + cc
+            x.far.at[cc, out_rows[k]], x.given.at[core, out_rows[k]], x.send_f.at[cc], x.recv_f.at[core, k], me, across + cc
         )
 
     def far_scale_copy(cc, k):
@@ -476,27 +522,25 @@
         )
 
     def mate_copy(k):
-        return remote(x.mate.at[rows_of[k]], x.mate_in.at[rows_of[k]], x.send_m, x.recv_m.at[k], me, partner)
-
-    def out_copy(k):
-        return pltpu.make_async_copy(x.out.at[:, rows_of[k]], out_hbm.at[0, :, rows_of[k]], x.sem_out.at[k])
+        return remote(x.mate.at[out_rows[k]], x.mate_in.at[out_rows[k]], x.send_m, x.recv_m.at[k], me, partner)
 
     def reduce_chunk(k):
         with jax.named_scope(f"gin_wait{k}"):
             for j in range(capacity):
                 if k == 0:
                     arrived(x.gin_scale.at[j], x.recv_gs.at[j])
-                arrived(x.gin.at[j, rows_of[k]], x.recv_g.at[j, k])
+                arrived(x.gin.at[j, out_rows[k]], x.recv_g.at[j, k])
+        start, size = out_cuts[k]
         targets = [stripe, partner, across, across + 1]
         sums = [[0.0] * 3 for _ in targets]
         for j in range(capacity):
             owner, _, row, col = slot_of(capacity * side + j)
             later = lax.rem(owner + 1, stripe_count)
-            here = row_index >= row - k * chunk
-            near = col_index >= col
+            here = rows_from(size) >= row - start
+            near = cols_from(size) >= col
             scale = x.gin_scale[j, k]
-            left = x.gin[j, rows_of[k], pl.ds(0, half)].astype(jnp.int32).astype(jnp.float32) * scale[:, :half]
-            mid = x.gin[j, rows_of[k], pl.ds(half, half)].astype(jnp.int32).astype(jnp.float32) * scale[:, half:]
+            left = x.gin[j, out_rows[k], pl.ds(0, half)].astype(jnp.int32).astype(jnp.float32) * scale[:, :half]
+            mid = x.gin[j, out_rows[k], pl.ds(half, half)].astype(jnp.int32).astype(jnp.float32) * scale[:, half:]
             pieces = (jnp.where(near, left, 0.0), mid, jnp.where(near, 0.0, left))
             for t, target in enumerate(targets):
                 gain = jnp.where(
@@ -509,35 +553,32 @@
                 lanes = pl.ds(place * half, half)
                 total = sums[2 + cc][place]
                 most = jnp.maximum(jnp.max(jnp.abs(total), axis=0, keepdims=True), 1e-30)
-                x.far[cc, rows_of[k], lanes] = jnp.round(total * (LEVELS / most)).astype(jnp.int32).astype(jnp.int16)
+                x.far[cc, out_rows[k], lanes] = jnp.round(total * (LEVELS / most)).astype(jnp.int32).astype(jnp.int16)
                 x.far_scale[cc, k, :, lanes] = most * (1.0 / LEVELS)
             far_copy(cc, k).start()
             far_scale_copy(cc, k).start()
         for place in range(3):
             lanes = pl.ds(place * half, half)
-            x.mate[rows_of[k], lanes] = sums[1][place]
-            x.own[rows_of[k], lanes] = sums[0][place]
+            x.mate[out_rows[k], lanes] = sums[1][place]
+            x.own[out_rows[k], lanes] = sums[0][place]
         mate_copy(k).start()
 
     def finish_chunk(k):
         with jax.named_scope(f"far_wait{k}"):
             for part in range(2):
-                arrived(x.given.at[part, rows_of[k]], x.recv_f.at[part, k])
+                arrived(x.given.at[part, out_rows[k]], x.recv_f.at[part, k])
                 arrived(x.given_scale.at[part, k], x.recv_fs.at[part, k])
-            arrived(x.mate_in.at[rows_of[k]], x.recv_m.at[k])
+            arrived(x.mate_in.at[out_rows[k]], x.recv_m.at[k])
         for part, base in ((core, x.own), (1 - core, x.mate_in)):
-            value = x.given[part, rows_of[k]].astype(jnp.int32).astype(jnp.float32)
-            x.out[part, rows_of[k]] = base[rows_of[k]] + value * x.given_scale[part, k]
-        out_copy(k).start()
-
-    for k in range(CHUNKS):
+            value = x.given[part, out_rows[k]].astype(jnp.int32).astype(jnp.float32)
+            out_ref[0, part, out_rows[k]] = base[out_rows[k]] + value * x.given_scale[part, k]
+
+    for k in range(outs):
         reduce_chunk(k)
         if k > 0:
             finish_chunk(k - 1)
-    finish_chunk(CHUNKS - 1)
-
-    for k in range(CHUNKS):
-        out_copy(k).wait()
+    finish_chunk(outs - 1)
+
     for cc in range(2):
         arrived(x.stage.at[cc], x.send_n.at[cc])
         arrived(x.far.at[cc], x.send_f.at[cc])
@@ -576,20 +617,25 @@
     length = probe_wave.shape[1]
     capacity = amplitudes.shape[0]
     assert layers == 1 and stripe_rows == length and 2 * width == 3 * length
-    assert depth_count >= capacity and stripe_count == 4
+    assert depth_count % 8 == 0 and stripe_count == 4 and capacity == 4
     items = scratch_list(depth_count, stripe_count, capacity, length, width, tables.shape[0] - 2)
-    smem = pl.BlockSpec(memory_space=pltpu.SMEM)
     sizes = (depth_count, stripe_count, capacity, length, width)
+    held = sum(
+        int(np.prod(shape.shape)) * jnp.dtype(shape.dtype).itemsize
+        for _, shape in items
+        if getattr(shape, "memory_space", None) == pltpu.VMEM
+    )
+    operands = (positions.T, counts, object_slices, probe_wave, amplitudes, tables)
     return pl.pallas_call(
         functools.partial(kernel, [name for name, _ in items], sizes),
-        out_shape=jax.ShapeDtypeStruct(object_slices.shape, jnp.float32),
-        in_specs=[smem] * 2 + [pl.BlockSpec(memory_space=pl.ANY)] * 4,
-        out_specs=pl.BlockSpec(memory_space=pl.ANY),
+        out_shape=pltpu.VMEM(object_slices.shape, jnp.float32),
+        in_specs=[pl.BlockSpec(memory_space=pl.ANY)] * len(operands),
+        out_specs=pl.BlockSpec(memory_space=pltpu.VMEM),
         scratch_shapes=[shape for _, shape in items],
         compiler_params=pltpu.CompilerParams(
-            collective_id=0, has_side_effects=True, vmem_limit_bytes=60 * 1024 * 1024
+            collective_id=0, has_side_effects=True, vmem_limit_bytes=held + (6 << 20)
         ),
-    )(positions.T, counts, object_slices, probe_wave, amplitudes, tables)
+    )(*(pltpu.with_memory_space_constraint(operand, pltpu.HBM) for operand in operands))
 
 
 def solution(mesh):

time: 61.1 us -> 52.8 us (0.86)
  the two profiles are of different devices: /device:TPU:1 before, /device:TPU:9 now
where the time goes in v2:
time: 52.8 us; the launch traced here: 52.7 us
  Pallas kernels  51.8 us (98%)
  local copies, waits for them, and re-layouts  0.88 us (2%)
    pallas_call x1, Pallas kernels, body(): pl.pallas_call(functools.partial(kernel, [name for name, _ in items], siz...  51.8 us

profile of v2, /device:TPU:9, one launch (start us, length us, event | category | flops | bytes accessed | tf_op | source)
XLA Modules:
  0.0 52.7 jit_solution(7797914329880311983)
XLA Ops:
  0.0 51.8 %shard_map.64 = f32[1,2,256,384]{3,2,1,0:T(8,128)S(1)} custom-call(s32[2,16]{1,0:T(2,128)} %bitcast.1, s32[4]{0:T(128)} %counts_hbm.1, f32[1,2,256,384]{3,2,1,0:T(8,128)} %object_hbm.1, bf16[2,256,256]{2,1,0:T(8,128)(2,1)} %probe_hbm.1, bf16[4,256,256]{2,1,0:T(8,128)(2,1)} %amp_hbm.1, bf16[18,256,256]{2,1,0:T(8,128)(2,1)} %constant.2.clone.table_hbm), custom_call_target="tpu_custom_call" | custom-call | tf_op jit(solution)/shard_map/pallas_call | solution.py:629
  51.8 0.9 %copy.8 = f32[1,2,256,384]{3,2,1,0:T(8,128)} copy(f32[1,2,256,384]{3,2,1,0:T(8,128)S(1)} %shard_map.64) | data formatting | bytes 1572864

commit v3 on v2

--- a/solution.py
+++ b/solution.py
@@ -13,8 +13,10 @@
 LEVELS = 32767.0
 IN_CUTS = (32, 64, 80, 80)
 OUT_CUTS = (64, 64, 64, 64)
-LATE = 4
+LATE = 6
 ORDER = (2, 3, 1, 0)
+UPPER_LAG = 0
+MIDDLE_LAG = 1
 MESH = pl.DeviceIdType.MESH
 
 
@@ -32,9 +34,9 @@
     first, second = prop[:half, :half], prop[:half, half:]
     parts = [(first + second) / 2, (first - second) / 2, dft[:half, 0::2], dft[:half, 1::2]]
     tables = []
-    for part in parts:
+    for place, part in enumerate(parts):
         right = right_form(part)
-        tables += [right, right.T]
+        tables += [right / LEVELS if place < 2 else right, right.T]
     stacked = np.stack(tables).astype(np.float32)
     high = stacked.astype(jnp.bfloat16)
     low = (stacked - high.astype(np.float32)).astype(jnp.bfloat16)
@@ -76,8 +78,8 @@
         ("win", pltpu.VMEM((capacity, length, length), jnp.int16)),
         ("wins", pltpu.VMEM((depth_count,) + field, jnp.int16)),
         ("waves", pltpu.VMEM((depth_count,) + field, jnp.float32)),
-        ("gout", pltpu.VMEM((depth_count,) + field, jnp.int16)),
-        ("gscale", pltpu.VMEM((depth_count, 2, outs, 1, length), jnp.float32)),
+        ("gout", pltpu.VMEM((2 * depth_count, length, length), jnp.int16)),
+        ("gscale", pltpu.VMEM((2 * depth_count, outs, 1, length), jnp.float32)),
         ("gin", pltpu.VMEM((capacity, length, length), jnp.int16)),
         ("gin_scale", pltpu.VMEM((capacity, outs, 1, length), jnp.float32)),
         ("rstack", pltpu.VMEM((count, 3 * length, length), jnp.bfloat16)),
@@ -99,24 +101,24 @@
         ("counts", pltpu.SMEM((stripe_count,), jnp.int32)),
         ("sem_s", dma((2,))),
         ("sem_obj", dma((ins,))),
-        ("sem_r", dma((count,))),
-        ("sem_l", dma((count,))),
+        ("sem_r", dma),
+        ("sem_l", dma),
         ("sem_p", dma((3,))),
         ("ready", regular((capacity,))),
-        ("send_n", dma((3,))),
-        ("recv_n", dma((ins, stripe_count))),
-        ("send_w", dma((capacity,))),
+        ("send_n", dma((2,))),
+        ("recv_n", dma((ins,))),
+        ("send_w", dma),
         ("recv_w", dma((depth_count,))),
         ("send_a", dma((2,))),
-        ("recv_a", dma((stripe_count,))),
-        ("send_g", dma((depth_count, 2))),
-        ("send_gs", dma((depth_count, 2))),
-        ("recv_g", dma((capacity, outs))),
-        ("recv_gs", dma((capacity,))),
-        ("send_f", dma((2,))),
-        ("send_fs", dma((2,))),
-        ("recv_f", dma((2, outs))),
-        ("recv_fs", dma((2, outs))),
+        ("recv_a", dma),
+        ("send_g", dma),
+        ("send_gs", dma),
+        ("recv_g", dma((outs,))),
+        ("recv_gs", dma),
+        ("send_f", dma),
+        ("send_fs", dma),
+        ("recv_f", dma((outs,))),
+        ("recv_fs", dma((outs,))),
         ("send_m", dma),
         ("recv_m", dma((outs,))),
     ]
@@ -205,8 +207,8 @@
             high, low = 2 * which, 2 * count + 2 * which
             for place, source in enumerate((high, low, high)):
                 span = pl.ds(place * length, length)
-                pltpu.make_async_copy(table_hbm.at[source], x.rstack.at[which, span], x.sem_r.at[which]).start()
-                pltpu.make_async_copy(table_hbm.at[source + 1], x.lstack.at[which, :, span], x.sem_l.at[which]).start()
+                pltpu.make_async_copy(table_hbm.at[source], x.rstack.at[which, span], x.sem_r).start()
+                pltpu.make_async_copy(table_hbm.at[source + 1], x.lstack.at[which, :, span], x.sem_l).start()
 
     def quantize(k):
         pltpu.make_async_copy(object_hbm.at[0, :, in_rows[k]], x.obj.at[:, in_rows[k]], x.sem_obj.at[k]).wait()
@@ -218,10 +220,10 @@
     def spread(k):
         for cc in range(2):
             remote(
-                x.stage.at[cc, in_rows[k]], slabs[k].at[stripe], x.send_n.at[cc], x.recv_n.at[k, stripe], me, across + cc
+                x.stage.at[cc, in_rows[k]], slabs[k].at[stripe], x.send_n.at[0], x.recv_n.at[k], me, across + cc
             ).start()
         remote(
-            x.stage.at[1 - core, in_rows[k]], slabs[k].at[stripe], x.send_n.at[2], x.recv_n.at[k, stripe], me, partner
+            x.stage.at[1 - core, in_rows[k]], slabs[k].at[stripe], x.send_n.at[1], x.recv_n.at[k], me, partner
         ).start()
 
     quantize(0)
@@ -252,16 +254,6 @@
             _, within, _, _ = slot_of(capacity * target + my_j)
             moved = dot(x.picks[0], x.amp[within]).astype(jnp.bfloat16)
             x.amp_send[target] = dot(moved, x.picks[1]).astype(jnp.bfloat16)
-
-            @pl.when(stripe == 2 * target)
-            def _():
-                pltpu.make_async_copy(x.amp_send.at[target], x.patterns.at[stripe], x.recv_a.at[stripe]).start()
-
-            @pl.when(stripe != 2 * target)
-            def _():
-                remote(
-                    x.amp_send.at[target], x.patterns.at[stripe], x.send_a.at[target], x.recv_a.at[stripe], me, 2 * target
-                ).start()
 
     my_owner, _, my_row, my_col = slot_of(capacity * side + my_j)
 
@@ -296,16 +288,14 @@
 
         @pl.when(jnp.logical_not(local(j)))
         def _():
-            remote(source, target, x.send_w.at[j], x.recv_w.at[me], workers[j], 2 * side).start()
+            remote(source, target, x.send_w, x.recv_w.at[me], workers[j], 2 * side).start()
 
         @pl.when(local(j))
         def _():
             pltpu.make_async_copy(source, target, x.recv_w.at[me]).start()
 
     def cut(k):
-        for step in range(1, stripe_count):
-            other = lax.rem(stripe + step, stripe_count)
-            arrived(slabs[k].at[other], x.recv_n.at[k, other])
+        arrived(slabs[k].at[pl.ds(0, stripe_count - 1)], x.recv_n.at[k])
         start, size = in_cuts[k]
         for j in order:
             owner, _, row, col = slot_of(capacity * side + j)
@@ -328,11 +318,37 @@
                 def _():
                     pl.semaphore_wait(x.ready.at[j], 1)
 
-    for k in range(ins):
-        with jax.named_scope(f"cut{k}"):
-            cut(k)
+    def lag_cases(j):
+        upper = me >= depth_count // 2
+        other = lax.rem(me + workers[j], 2) == 1
+        middle = (me >= depth_count // 4) & jnp.logical_not(upper) & (workers[j] >= depth_count // 2)
+        held = upper & other
+        plain = jnp.logical_not(held | middle)
+        return [(0, plain), (UPPER_LAG, held), (MIDDLE_LAG, middle)]
+
+    for step in range(ins + max(UPPER_LAG, MIDDLE_LAG)):
+        if step < ins:
+            with jax.named_scope(f"cut{step}"):
+                cut(step)
         for j in order:
-            window_send(j, in_rows[k])
+            for lag, here in lag_cases(j):
+                if 0 <= step - lag < ins:
+                    @pl.when(here)
+                    def _():
+                        window_send(j, in_rows[step - lag])
+
+    @pl.when(in_plane)
+    def _():
+        for target in range(2):
+            @pl.when(stripe == 2 * target)
+            def _():
+                pltpu.make_async_copy(x.amp_send.at[target], x.patterns.at[stripe], x.recv_a).start()
+
+            @pl.when(stripe != 2 * target)
+            def _():
+                remote(
+                    x.amp_send.at[target], x.patterns.at[stripe], x.send_a.at[target], x.recv_a, me, 2 * target
+                ).start()
 
     def right_dot(value, which):
         high, low = parts_of(value)
@@ -373,7 +389,7 @@
         return join_rows(left_dot(0, u), left_dot(1, v))
 
     def window_of(layer):
-        value = x.wins[layer].astype(jnp.int32).astype(jnp.float32) * (1.0 / LEVELS)
+        value = x.wins[layer].astype(jnp.int32).astype(jnp.float32)
         return value[0], value[1]
 
     def gradient_copies(layer, k, action):
@@ -382,8 +398,8 @@
             def _():
                 action(
                     remote(
-                        x.gout.at[layer, part, out_rows[k]], x.gin.at[my_j, out_rows[k]], x.send_g.at[layer, part],
-                        x.recv_g.at[my_j, k], layer, 2 * side + part,
+                        x.gout.at[2 * layer + part, out_rows[k]], x.gin.at[my_j, out_rows[k]], x.send_g,
+                        x.recv_g.at[k], layer, 2 * side + part,
                     )
                 )
 
@@ -391,7 +407,7 @@
         def _():
             action(
                 pltpu.make_async_copy(
-                    x.gout.at[layer, 0, out_rows[k]], x.gin.at[my_j, out_rows[k]], x.recv_g.at[my_j, k]
+                    x.gout.at[2 * layer, out_rows[k]], x.gin.at[my_j, out_rows[k]], x.recv_g.at[k]
                 )
             )
 
@@ -401,12 +417,12 @@
                 start, size = out_cuts[k]
                 piece = value[start : start + size]
                 most = jnp.maximum(jnp.max(jnp.abs(piece), axis=0, keepdims=True), 1e-30)
-                x.gout[layer, part, out_rows[k]] = jnp.round(piece * (LEVELS / most)).astype(jnp.int32).astype(jnp.int16)
-                x.gscale[layer, part, k] = most * (1.0 / LEVELS)
+                x.gout[2 * layer + part, out_rows[k]] = jnp.round(piece * (LEVELS / most)).astype(jnp.int32).astype(jnp.int16)
+                x.gscale[2 * layer + part, k] = most * (1.0 / LEVELS)
 
         def scale_copy(part):
             return remote(
-                x.gscale.at[layer, part], x.gin_scale.at[my_j], x.send_gs.at[layer, part], x.recv_gs.at[my_j], layer,
+                x.gscale.at[2 * layer + part], x.gin_scale.at[my_j], x.send_gs, x.recv_gs, layer,
                 2 * side + part,
             )
 
@@ -416,7 +432,7 @@
 
         @pl.when(layer == me)
         def _():
-            pltpu.make_async_copy(x.gscale.at[layer, 0], x.gin_scale.at[my_j], x.recv_gs.at[my_j]).start()
+            pltpu.make_async_copy(x.gscale.at[2 * layer], x.gin_scale.at[my_j], x.recv_gs).start()
 
         scale_copy(1).start()
         for k in range(outs):
@@ -428,9 +444,8 @@
 
     @pl.when(is_worker)
     def _():
-        for which in range(count):
-            arrived(x.rstack.at[which], x.sem_r.at[which])
-            arrived(x.lstack.at[which], x.sem_l.at[which])
+        arrived(x.rstack, x.sem_r)
+        arrived(x.lstack, x.sem_l)
 
         @pl.loop(0, depth_count - 1)
         def forward(layer):
@@ -447,8 +462,8 @@
             arrived(x.wins.at[last], x.recv_w.at[last])
         win_re, win_im = window_of(last)
         wave_re, wave_im = x.waves[last, 0], x.waves[last, 1]
-        re = wave_re * win_re - wave_im * win_im
-        im = wave_re * win_im + wave_im * win_re
+        re = (wave_re * win_re - wave_im * win_im) * (1.0 / LEVELS)
+        im = (wave_re * win_im + wave_im * win_re) * (1.0 / LEVELS)
         u, v = split_lanes(re, im)
         even, odd = right_dot(u, 2), right_dot(v, 3)
         re = jnp.concatenate([even[:, :half], odd[:, :half]], axis=1)
@@ -456,8 +471,7 @@
         u, v = split_rows(re, im)
         even, odd = left_dot(2, u), left_dot(3, v)
         with jax.named_scope("amp_wait"):
-            for source in range(stripe_count):
-                arrived(x.patterns.at[source], x.recv_a.at[source])
+            arrived(x.patterns, x.recv_a)
         amp = x.patterns[my_owner].astype(jnp.float32)
         re = jnp.concatenate([even[:half], odd[:half]], axis=0)
         im = jnp.concatenate([even[half:], odd[half:]], axis=0)
@@ -513,12 +527,12 @@
 
     def far_copy(cc, k):
         return remote(
-            x.far.at[cc, out_rows[k]], x.given.at[core, out_rows[k]], x.send_f.at[cc], x.recv_f.at[core, k], me, across + cc
+            x.far.at[cc, out_rows[k]], x.given.at[core, out_rows[k]], x.send_f, x.recv_f.at[k], me, across + cc
         )
 
     def far_scale_copy(cc, k):
         return remote(
-            x.far_scale.at[cc, k], x.given_scale.at[core, k], x.send_fs.at[cc], x.recv_fs.at[core, k], me, across + cc
+            x.far_scale.at[cc, k], x.given_scale.at[core, k], x.send_fs, x.recv_fs.at[k], me, across + cc
         )
 
     def mate_copy(k):
@@ -526,10 +540,9 @@
 
     def reduce_chunk(k):
         with jax.named_scope(f"gin_wait{k}"):
-            for j in range(capacity):
-                if k == 0:
-                    arrived(x.gin_scale.at[j], x.recv_gs.at[j])
-                arrived(x.gin.at[j, out_rows[k]], x.recv_g.at[j, k])
+            if k == 0:
+                arrived(x.gin_scale, x.recv_gs)
+            arrived(x.gin.at[:, out_rows[k]], x.recv_g.at[k])
         start, size = out_cuts[k]
         targets = [stripe, partner, across, across + 1]
         sums = [[0.0] * 3 for _ in targets]
@@ -565,9 +578,8 @@
 
     def finish_chunk(k):
         with jax.named_scope(f"far_wait{k}"):
-            for part in range(2):
-                arrived(x.given.at[part, out_rows[k]], x.recv_f.at[part, k])
-                arrived(x.given_scale.at[part, k], x.recv_fs.at[part, k])
+            arrived(x.given.at[:, out_rows[k]], x.recv_f.at[k])
+            arrived(x.given_scale.at[:, k], x.recv_fs.at[k])
             arrived(x.mate_in.at[out_rows[k]], x.recv_m.at[k])
         for part, base in ((core, x.own), (1 - core, x.mate_in)):
             value = x.given[part, out_rows[k]].astype(jnp.int32).astype(jnp.float32)
@@ -579,16 +591,18 @@
             finish_chunk(k - 1)
     finish_chunk(outs - 1)
 
-    for cc in range(2):
-        arrived(x.stage.at[cc], x.send_n.at[cc])
-        arrived(x.far.at[cc], x.send_f.at[cc])
-        arrived(x.far_scale.at[cc], x.send_fs.at[cc])
-    arrived(x.stage.at[0], x.send_n.at[2])
+    arrived(x.stage, x.send_n.at[0])
+    arrived(x.stage.at[0], x.send_n.at[1])
+    arrived(x.far, x.send_f)
+    arrived(x.far_scale, x.send_fs)
     arrived(x.mate, x.send_m)
-    for j, worker in enumerate(workers):
-        @pl.when(jnp.logical_not((me == worker) & (core == 0)))
-        def _():
-            arrived(x.win.at[j], x.send_w.at[j])
+    @pl.when(is_worker)
+    def _():
+        arrived(x.win.at[pl.ds(0, capacity - 1)], x.send_w)
+
+    @pl.when(jnp.logical_not(is_worker))
+    def _():
+        arrived(x.win, x.send_w)
 
     @pl.when(in_plane)
     def _():
@@ -599,15 +613,8 @@
 
     @pl.when(is_worker)
     def _():
-        @pl.loop(0, depth_count)
-        def _(layer):
-            arrived(x.gout.at[layer, 1], x.send_g.at[layer, 1])
-            arrived(x.gscale.at[layer, 1], x.send_gs.at[layer, 1])
-
-            @pl.when(layer != me)
-            def _():
-                arrived(x.gout.at[layer, 0], x.send_g.at[layer, 0])
-                arrived(x.gscale.at[layer, 0], x.send_gs.at[layer, 0])
+        arrived(x.gout.at[pl.ds(0, 2 * depth_count - 1)], x.send_g)
+        arrived(x.gscale.at[pl.ds(0, 2 * depth_count - 1)], x.send_gs)
 
 
 def body(tables, object_slices, probe_wave, amplitudes, positions, counts):

time: 52.8 us -> 51.2 us (0.970)
  the two profiles are of different devices: /device:TPU:9 before, /device:TPU:1 now
where the time goes in v3:
time: 51.2 us; the launch traced here: 51.1 us
  Pallas kernels  50.2 us (98%)
  local copies, waits for them, and re-layouts  0.88 us (2%)
    pallas_call x1, Pallas kernels, body(): pl.pallas_call(functools.partial(kernel, [name for name, _ in items], siz...  50.2 us

profile of v3, /device:TPU:1, one launch (start us, length us, event | category | flops | bytes accessed | tf_op | source)
XLA Modules:
  0.0 51.1 jit_solution(14875631929172693616)
XLA Ops:
  0.0 50.2 %shard_map.64 = f32[1,2,256,384]{3,2,1,0:T(8,128)S(1)} custom-call(s32[2,16]{1,0:T(2,128)} %bitcast.1, s32[4]{0:T(128)} %counts_hbm.1, f32[1,2,256,384]{3,2,1,0:T(8,128)} %object_hbm.1, bf16[2,256,256]{2,1,0:T(8,128)(2,1)} %probe_hbm.1, bf16[4,256,256]{2,1,0:T(8,128)(2,1)} %amp_hbm.1, bf16[18,256,256]{2,1,0:T(8,128)(2,1)} %constant.2.clone.table_hbm), custom_call_target="tpu_custom_call" | custom-call | tf_op jit(solution)/shard_map/pallas_call | solution.py:636
  50.2 0.9 %copy.8 = f32[1,2,256,384]{3,2,1,0:T(8,128)} copy(f32[1,2,256,384]{3,2,1,0:T(8,128)S(1)} %shard_map.64) | data formatting | bytes 1572864

commit v4 on v3

--- a/solution.py
+++ b/solution.py
@@ -11,9 +11,9 @@
 
 smoothing = 0.25
 LEVELS = 32767.0
-IN_CUTS = (32, 64, 80, 80)
+IN_CUTS = (48, 64, 80, 64)
 OUT_CUTS = (64, 64, 64, 64)
-LATE = 6
+LATE = 5
 ORDER = (2, 3, 1, 0)
 UPPER_LAG = 0
 MIDDLE_LAG = 1
@@ -544,8 +544,7 @@
                 arrived(x.gin_scale, x.recv_gs)
             arrived(x.gin.at[:, out_rows[k]], x.recv_g.at[k])
         start, size = out_cuts[k]
-        targets = [stripe, partner, across, across + 1]
-        sums = [[0.0] * 3 for _ in targets]
+        terms = []
         for j in range(capacity):
             owner, _, row, col = slot_of(capacity * side + j)
             later = lax.rem(owner + 1, stripe_count)
@@ -554,27 +553,31 @@
             scale = x.gin_scale[j, k]
             left = x.gin[j, out_rows[k], pl.ds(0, half)].astype(jnp.int32).astype(jnp.float32) * scale[:, :half]
             mid = x.gin[j, out_rows[k], pl.ds(half, half)].astype(jnp.int32).astype(jnp.float32) * scale[:, half:]
-            pieces = (jnp.where(near, left, 0.0), mid, jnp.where(near, 0.0, left))
-            for t, target in enumerate(targets):
+            terms.append((owner, later, here, (jnp.where(near, left, 0.0), mid, jnp.where(near, 0.0, left))))
+
+        def sums_for(target):
+            sums = [0.0] * 3
+            for owner, later, here, pieces in terms:
                 gain = jnp.where(
                     here, jnp.where(owner == target, 1.0, 0.0), jnp.where(later == target, 1.0, 0.0)
                 )
                 for place, piece in enumerate(pieces):
-                    sums[t][place] = sums[t][place] + piece * gain
+                    sums[place] = sums[place] + piece * gain
+            return sums
+
         for cc in range(2):
-            for place in range(3):
+            for place, total in enumerate(sums_for(across + cc)):
                 lanes = pl.ds(place * half, half)
-                total = sums[2 + cc][place]
                 most = jnp.maximum(jnp.max(jnp.abs(total), axis=0, keepdims=True), 1e-30)
                 x.far[cc, out_rows[k], lanes] = jnp.round(total * (LEVELS / most)).astype(jnp.int32).astype(jnp.int16)
                 x.far_scale[cc, k, :, lanes] = most * (1.0 / LEVELS)
             far_copy(cc, k).start()
             far_scale_copy(cc, k).start()
-        for place in range(3):
-            lanes = pl.ds(place * half, half)
-            x.mate[out_rows[k], lanes] = sums[1][place]
-            x.own[out_rows[k], lanes] = sums[0][place]
+        for place, total in enumerate(sums_for(partner)):
+            x.mate[out_rows[k], pl.ds(place * half, half)] = total
         mate_copy(k).start()
+        for place, total in enumerate(sums_for(stripe)):
+            x.own[out_rows[k], pl.ds(place * half, half)] = total
 
     def finish_chunk(k):
         with jax.named_scope(f"far_wait{k}"):
@@ -587,9 +590,8 @@
 
     for k in range(outs):
         reduce_chunk(k)
-        if k > 0:
-            finish_chunk(k - 1)
-    finish_chunk(outs - 1)
+    for k in range(outs):
+        finish_chunk(k)
 
     arrived(x.stage, x.send_n.at[0])
     arrived(x.stage.at[0], x.send_n.at[1])

time: 51.2 us -> 51.1 us (level)
  no operation moved by 1% of the time
where the time goes in v4:
time: 51.1 us; the launch traced here: 51 us
  Pallas kernels  50.1 us (98%)
  local copies, waits for them, and re-layouts  0.88 us (2%)
    pallas_call x1, Pallas kernels, body(): pl.pallas_call(functools.partial(kernel, [name for name, _ in items], siz...  50.1 us

profile of v4, /device:TPU:1, one launch (start us, length us, event | category | flops | bytes accessed | tf_op | source)
XLA Modules:
  0.0 51.0 jit_solution(11819201422623960414)
XLA Ops:
  0.0 50.1 %shard_map.64 = f32[1,2,256,384]{3,2,1,0:T(8,128)S(1)} custom-call(s32[2,16]{1,0:T(2,128)} %bitcast.1, s32[4]{0:T(128)} %counts_hbm.1, f32[1,2,256,384]{3,2,1,0:T(8,128)} %object_hbm.1, bf16[2,256,256]{2,1,0:T(8,128)(2,1)} %probe_hbm.1, bf16[4,256,256]{2,1,0:T(8,128)(2,1)} %amp_hbm.1, bf16[18,256,256]{2,1,0:T(8,128)(2,1)} %constant.2.clone.table_hbm), custom_call_target="tpu_custom_call" | custom-call | tf_op jit(solution)/shard_map/pallas_call | solution.py:638
  50.1 0.9 %copy.8 = f32[1,2,256,384]{3,2,1,0:T(8,128)} copy(f32[1,2,256,384]{3,2,1,0:T(8,128)S(1)} %shard_map.64) | data formatting | bytes 1572864
